TPU v7x, 32 devices: a whole 2x2x4 slice. The times are simulated.
32 devices in a mesh: polar: 4 (over y, x), azimuth: 8 (over z, core).
Axes of the slice: x: 2, y: 2, z: 4, core: 2. Of those that a mesh axis runs over, the one named last changes fastest.
Arguments:
- grid_state: bfloat16 [32, 512, 640], P('polar', 'azimuth'), may hold values from -6 to 6
- filter_taps: bfloat16 [32, 9, 4, 129], P('polar'), may hold values from -0.59765625 to 0.59765625
- support_start: int32 [32], P('polar'), may hold values from -64 to 64, as said below
- support_count: int32 [32], P('polar'), may hold values from 1 to 129
- filter_mix: bfloat16 [2, 9, 640], replicated, may hold values from -2 to 2
- w_in: bfloat16 [2, 640, 1280], replicated, may hold values from -0.25 to 0.25
- w_out: bfloat16 [2, 1280, 640], replicated, may hold values from -0.15625 to 0.15625
Outputs:
- next_state: bfloat16 [32, 512, 640], P('polar', 'azimuth')
Inputs may be any that keep to these rules, and one draw needn't show every extreme that they name: support_start[i] + support_count[i] - 1 <= 64; support is widest near the poles.
All inputs are finite; a program needn't handle non-finite values.
Results may differ from a plain program's by a relative error of at most 0.006.
Values may be sent and summed in bfloat16 or wider, within the bound.
No kernel may reach another device: no remote copies, remote signals or barrier semaphores. Data moves between devices by JAX's collectives and lax.ppermute only.
A program may use at most 64 MiB of HBM per device.

v0:
```python
import jax
import jax.numpy as jnp
from jax import lax
from jax.sharding import PartitionSpec as P


def from_behind(block, axis, distance):
    devices = range(lax.axis_size(axis))
    route = [(i - distance, i) for i in devices if i - distance in devices]
    return lax.ppermute(block, axis, route)


def padded(block, sides, width):
    for axis, dim in sides:
        count = lax.axis_size(axis)
        forward = [(i, i + 1) for i in range(count - 1)]
        forward.append((count - 1, 0))
        backward = [(target, source) for source, target in forward]
        low = lax.ppermute(
            lax.slice_in_dim(block, block.shape[dim] - width, None, axis=dim), axis, forward
        )
        high = lax.ppermute(lax.slice_in_dim(block, 0, width, axis=dim), axis, backward)
        block = jnp.concatenate([low, block, high], axis=dim)
    return block


def tap_bands(filter_taps, support_start, support_count, reach):
    tap_count = filter_taps.shape[-1]
    offsets = jnp.arange(tap_count, dtype=jnp.int32) - reach
    inside = (offsets[None, :] >= support_start[:, None]) & (
        offsets[None, :] < (support_start + support_count)[:, None]
    )
    masked = jnp.where(inside[:, None, None, :], filter_taps.astype(jnp.float32), jnp.float32(0.0))
    column = jnp.arange(reach, dtype=jnp.int32)[:, None]
    window = jnp.arange(3 * reach, dtype=jnp.int32)[None, :]
    onehot = (
        (window - column)[:, :, None] == jnp.arange(tap_count, dtype=jnp.int32)[None, None, :]
    ).astype(jnp.float32)
    return jnp.einsum("akrt,jwt->akjrw", masked, onehot).astype(jnp.bfloat16)


def channel_mlp(act, field, first, second):
    flat = act.reshape(-1, act.shape[-1])
    hidden = jax.nn.gelu(
        jnp.dot(flat, first, preferred_element_type=jnp.float32), approximate=False
    ).astype(jnp.bfloat16)
    update = jnp.dot(hidden, second, preferred_element_type=jnp.float32)
    return (field.astype(jnp.float32) + update.reshape(field.shape)).astype(jnp.bfloat16)


def shards(grid_state, filter_taps, support_start, support_count, filter_mix, w_in, w_out):
    lat_rows = grid_state.shape[0]
    reach = grid_state.shape[1]
    bands = tap_bands(filter_taps, support_start, support_count, reach)
    field = grid_state
    for layer_no in range(w_in.shape[0]):
        above = from_behind(field[-2:], "polar", 1)
        below = from_behind(field[:1], "polar", -1)
        extended = jnp.concatenate([above, field, below], axis=0)
        mix_row = filter_mix[layer_no].astype(jnp.float32)
        wide = padded(extended, (("azimuth", 1),), reach)
        stacked = jnp.stack([wide[lat_no : lat_no + 4] for lat_no in range(lat_rows)])
        conv = jnp.einsum("akjrw,arwc->akjc", bands, stacked, preferred_element_type=jnp.float32)
        mixed = jnp.einsum("akjc,kc->ajc", conv, mix_row)
        act = jax.nn.gelu(mixed, approximate=False).astype(jnp.bfloat16)
        field = channel_mlp(act, field, w_in[layer_no], w_out[layer_no])
    return field


def solution(mesh):
    return jax.shard_map(
        shards,
        mesh=mesh,
        in_specs=(
            P("polar", "azimuth", None),
            P("polar", None, None, None),
            P("polar"),
            P("polar"),
            P(),
            P(),
            P(),
        ),
        out_specs=P("polar", "azimuth", None),
        check_vma=False,
    )
```

profile of v0, /device:TPU:1, one launch (start us, length us, event | category | flops | bytes accessed | tf_op | source)
XLA Modules:
  0.0 146.0 jit_solution(6529809046132100774)
XLA Ops:
  0.0 0.0 copy-start.1
  0.0 1.0 slice.78
  1.0 3.9 %collective-permute-start = (bf16[2,64,640]{2,1,0:T(8,128)(2,1)S(1)}, bf16[2,64,640]{2,1,0:T(8,128)(2,1)S(1)}, u32[]{:S(2)}, u32[]{:S(2)}) collective-permute-start(bf16[2,64,640]{2,1,0:T(8,128)(2,1)S(1)} %slice.78), channel_id=1, source_target_pairs={{0,8},{8,16},{16,24},{1,9},{9,17},{17,25},{2,10},{10,18},{18,26},{... | collective-permute-start | bytes 491528 | tf_op jit(solution)/shard_map/ppermute | solution.py:10
  4.9 0.9 slice.79
  5.8 1.3 collective-permute-start.1
  7.1 1.5 fusion.121
  8.6 0.6 bitcast_convert_fusion.1
  9.2 0.7 add.14
  9.9 0.7 compare_and_fusion
  10.6 0.0 collective-permute-done
  10.6 1.2 constant_dynamic-update-slice_fusion.1
  11.8 0.0 collective-permute-done.1
  11.8 2.5 %collective-permute-start.2 = (bf16[11,64,640]{2,1,0:T(8,128)(2,1)S(1)}, bf16[11,64,640]{2,1,0:T(8,128)(2,1)}, u32[]{:S(2)}, u32[]{:S(2)}) collective-permute-start(bf16[11,64,640]{2,1,0:T(8,128)(2,1)S(1)} %constant_dynamic-update-slice_fusion), channel_id=1, source_target_pairs={{0,1},{1,2},{2,3},{3,4},{4,5},{5,6},{6,7},{7,0},{8,9},{9,10},{10,1... | collective-permute-start | bytes 2703368 | tf_op jit(solution)/shard_map/ppermute | solution.py:19
  14.3 0.0 collective-permute-start.3
  14.4 0.6 iota_subtract_fusion
  15.0 0.0 copy-done.1
  15.0 0.1 convert_select_fusion
  15.1 5.6 %convert_bitcast_fusion = bf16[8,9,64,4,192]{4,1,3,0,2:T(8,128)(2,1)S(1)} fusion(s32[64,192]{1,0:T(8,128)} %iota_subtract_fusion, bf16[8,9,4,129]{3,2,1,0:T(4,128)(2,1)S(1)} %convert_select_fusion), kind=kOutput, calls=%fused_computation | convolution fusion | flops 914632704 | bytes 7201344 | tf_op jit(solution)/shard_map/akrt,jwt->akjrw/dot_general | solution.py:39
  20.7 11.0 %collective-permute-done.2 = bf16[11,64,640]{2,1,0:T(8,128)(2,1)} collective-permute-done((bf16[11,64,640]{2,1,0:T(8,128)(2,1)S(1)}, bf16[11,64,640]{2,1,0:T(8,128)(2,1)}, u32[]{:S(2)}, u32[]{:S(2)}) %collective-permute-start.2) | collective-permute-done | bytes 901152 | tf_op jit(solution)/shard_map/ppermute | solution.py:19
  31.6 5.1 %collective-permute-done.3 = bf16[11,64,640]{2,1,0:T(8,128)(2,1)} collective-permute-done((bf16[11,64,640]{2,1,0:T(8,128)(2,1)S(1)}, bf16[11,64,640]{2,1,0:T(8,128)(2,1)}, u32[]{:S(2)}, u32[]{:S(2)}) %collective-permute-start.3) | collective-permute-done | bytes 901152 | tf_op jit(solution)/shard_map/ppermute | solution.py:22
  36.7 1.7 %pad_maximum_fusion = bf16[11,192,640]{2,1,0:T(8,128)(2,1)S(1)} fusion(bf16[11,64,640]{2,1,0:T(8,128)(2,1)} %collective-permute-done.3, bf16[11,64,640]{2,1,0:T(8,128)(2,1)S(1)} %constant_dynamic-update-slice_fusion, bf16[11,64,640]{2,1,0:T(8,128)(2,1)} %collective-permute-done.2), kind=kLoop, calls=%fused_computation.16 | loop fusion | flops 8110080 | bytes 5406720 | tf_op jit(solution)/shard_map/concatenate | solution.py:23
  38.4 1.0 fusion.118
  39.4 1.1 fusion.117
  40.5 1.0 fusion.116
  41.5 1.0 fusion.115
  42.6 1.0 fusion.114
  43.6 1.1 fusion.113
  44.7 1.0 fusion.112
  45.7 1.0 fusion.111
  46.8 0.0 copy-done.3
  46.8 13.4 %fusion.1 = f32[640,8,64]{0,2,1:T(8,128)} fusion(f32[640,9]{0,1:T(8,128)S(1)} %copy-done.3, bf16[8,4,192,640]{3,2,1,0:T(8,128)(2,1)} %fusion.111, bf16[8,9,64,4,192]{4,1,3,0,2:T(8,128)(2,1)S(1)} %convert_bitcast_fusion), kind=kOutput, calls=%fused_computation.4 | convolution fusion | flops 4535418880 | bytes 16275968 | tf_op jit(solution)/shard_map/akjrw,arwc->akjc/dot_general | solution.py:63
  60.1 4.0 %fusion.69 = bf16[8,64,640]{2,1,0:T(8,128)(2,1)S(1)} fusion(f32[640,8,64]{0,2,1:T(8,128)} %fusion.1), kind=kLoop, calls=%fused_computation.74 | loop fusion | flops 21299200 | bytes 1966080 | tf_op jit(solution)/shard_map/convert_element_type | solution.py:65
  64.1 0.0 copy-start
  64.1 0.0 copy-start.4
  64.1 7.9 %fusion.13 = bf16[512,1280]{1,0:T(8,128)(2,1)S(1)} fusion(bf16[512,640]{1,0:T(8,128)(2,1)S(1)} %bitcast.272, bf16[2,640,1280]{2,1,0:T(8,128)(2,1)} %param.12), kind=kOutput, calls=%fused_computation.20 | convolution fusion | flops 881459200 | bytes 3604480 | tf_op jit(solution)/shard_map/dot_general | solution.py:45
  72.0 0.0 copy-done
  72.0 0.0 copy-done.4
  72.0 0.0 copy-start.2
  72.0 1.2 fusion.64
  73.2 4.0 %collective-permute-start.4 = (bf16[2,64,640]{2,1,0:T(8,128)(2,1)S(1)}, bf16[2,64,640]{2,1,0:T(8,128)(2,1)S(1)}, u32[]{:S(2)}, u32[]{:S(2)}) collective-permute-start(bf16[2,64,640]{2,1,0:T(8,128)(2,1)S(1)} %slice.112), channel_id=1, source_target_pairs={{0,8},{8,16},{16,24},{1,9},{9,17},{17,25},{2,10},{10,18},{18,26},{... | collective-permute-start | bytes 491528 | tf_op jit(solution)/shard_map/ppermute | solution.py:10
  77.3 1.3 collective-permute-start.5
  78.6 6.0 %collective-permute-done.5 = bf16[1,64,640]{2,1,0:T(8,128)(2,1)S(1)} collective-permute-done((bf16[1,64,640]{2,1,0:T(8,128)(2,1)S(1)}, bf16[1,64,640]{2,1,0:T(8,128)(2,1)S(1)}, u32[]{:S(2)}, u32[]{:S(2)}) %collective-permute-start.5) | collective-permute-done | bytes 81952 | tf_op jit(solution)/shard_map/ppermute | solution.py:10
  84.5 0.0 collective-permute-done.4
  84.5 0.1 pad_maximum_fusion.2
  84.7 1.9 %collective-permute-start.6 = (bf16[11,64,640]{2,1,0:T(8,128)(2,1)S(1)}, bf16[11,64,640]{2,1,0:T(8,128)(2,1)S(1)}, u32[]{:S(2)}, u32[]{:S(2)}) collective-permute-start(bf16[11,64,640]{2,1,0:T(8,128)(2,1)S(1)} %pad_maximum_fusion.2), channel_id=1, source_target_pairs={{0,1},{1,2},{2,3},{3,4},{4,5},{5,6},{6,7},{7,0},{8,9},{9,10},{10,1... | collective-permute-start | bytes 2703368 | tf_op jit(solution)/shard_map/ppermute | solution.py:19
  86.5 0.0 collective-permute-start.7
  86.5 0.0 copy-done.2
  86.6 18.1 %collective-permute-done.6 = bf16[11,64,640]{2,1,0:T(8,128)(2,1)S(1)} collective-permute-done((bf16[11,64,640]{2,1,0:T(8,128)(2,1)S(1)}, bf16[11,64,640]{2,1,0:T(8,128)(2,1)S(1)}, u32[]{:S(2)}, u32[]{:S(2)}) %collective-permute-start.6) | collective-permute-done | bytes 901152 | tf_op jit(solution)/shard_map/ppermute | solution.py:19
  104.7 3.2 %collective-permute-done.7 = bf16[11,64,640]{2,1,0:T(8,128)(2,1)S(1)} collective-permute-done((bf16[11,64,640]{2,1,0:T(8,128)(2,1)S(1)}, bf16[11,64,640]{2,1,0:T(8,128)(2,1)S(1)}, u32[]{:S(2)}, u32[]{:S(2)}) %collective-permute-start.7) | collective-permute-done | bytes 901152 | tf_op jit(solution)/shard_map/ppermute | solution.py:22
  107.9 2.6 %pad_maximum_fusion.1 = bf16[11,192,640]{2,1,0:T(8,128)(2,1)S(1)} fusion(bf16[11,64,640]{2,1,0:T(8,128)(2,1)S(1)} %collective-permute-done.7, bf16[1,64,640]{2,1,0:T(8,128)(2,1)S(1)} %collective-permute-done.5, bf16[8,64,640]{2,1,0:T(8,128)(2,1)S(1)} %fusion.64, bf16[2,64,640]{2,1,0:T(8,128)(2,1)S(1)} %collective-permute-done.4, ...), kind=kLoop, calls=%fused_computation.17 | loop fusion | flops 13516800 | bytes 5406720 | tf_op jit(solution)/shard_map/concatenate | solution.py:23
  110.5 1.0 fusion.110
  111.5 1.1 fusion.109
  112.6 1.0 fusion.108
  113.7 1.0 fusion.107
  114.7 1.0 fusion.106
  115.7 1.1 fusion.105
  116.8 1.0 fusion.104
  117.8 1.0 fusion.103
  118.9 13.4 %fusion = f32[640,8,64]{0,2,1:T(8,128)} fusion(f32[640,9]{0,1:T(8,128)S(1)} %bitcast_convert_fusion, bf16[8,4,192,640]{3,2,1,0:T(8,128)(2,1)} %fusion.103, bf16[8,9,64,4,192]{4,1,3,0,2:T(8,128)(2,1)S(1)} %convert_bitcast_fusion), kind=kOutput, calls=%fused_computation.2 | convolution fusion | flops 4535418880 | bytes 16275968 | tf_op jit(solution)/shard_map/akjrw,arwc->akjc/dot_general | solution.py:63
  132.2 4.0 %fusion.72 = bf16[8,64,640]{2,1,0:T(8,128)(2,1)S(1)} fusion(f32[640,8,64]{0,2,1:T(8,128)} %fusion), kind=kLoop, calls=%fused_computation.77 | loop fusion | flops 21299200 | bytes 1966080 | tf_op jit(solution)/shard_map/convert_element_type | solution.py:65
  136.2 0.0 copy-start.5
  136.2 7.7 %fusion.16 = bf16[512,1280]{1,0:T(8,128)(2,1)S(1)} fusion(bf16[512,640]{1,0:T(8,128)(2,1)S(1)} %bitcast.273, bf16[2,640,1280]{2,1,0:T(8,128)(2,1)} %param.12), kind=kOutput, calls=%fused_computation.23 | convolution fusion | flops 881459200 | bytes 3604480 | tf_op jit(solution)/shard_map/dot_general | solution.py:45
  143.9 0.0 copy-done.5
  143.9 2.0 %fusion.61 = bf16[8,64,640]{2,1,0:T(8,128)(2,1)} fusion(bf16[8,64,1280]{2,1,0:T(8,128)(2,1)S(1)} %bitcast.274, bf16[2,1280,640]{2,1,0:T(8,128)(2,1)S(1)} %copy-done.5, bf16[8,64,640]{2,1,0:T(8,128)(2,1)S(1)} %fusion.64), kind=kOutput, calls=%fused_computation.70 | convolution fusion | flops 839843840 | bytes 4259840 | tf_op jit(solution)/shard_map/dot_general | solution.py:47
  (7 shorter events, 0.1 us)
Async XLA Ops:
  0.0 15.0 %copy-start.1 = (bf16[8,9,4,129]{3,2,1,0:T(4,128)(2,1)S(1)}, bf16[8,9,4,129]{3,2,1,0:T(4,128)(2,1)}, u32[]{:S(2)}) copy-start(bf16[8,9,4,129]{3,2,1,0:T(4,128)(2,1)} %param.8) | copy-start | bytes 222916
  1.0 9.6 %collective-permute-start = (bf16[2,64,640]{2,1,0:T(8,128)(2,1)S(1)}, bf16[2,64,640]{2,1,0:T(8,128)(2,1)S(1)}, u32[]{:S(2)}, u32[]{:S(2)}) collective-permute-start(bf16[2,64,640]{2,1,0:T(8,128)(2,1)S(1)} %slice.78), channel_id=1, source_target_pairs={{0,8},{8,16},{16,24},{1,9},{9,17},{17,25},{2,10},{10,18},{18,26},{... | collective-permute-start | bytes 491528 | tf_op jit(solution)/shard_map/ppermute | solution.py:10
  5.8 6.0 %collective-permute-start.1 = (bf16[1,64,640]{2,1,0:T(8,128)(2,1)S(1)}, bf16[1,64,640]{2,1,0:T(8,128)(2,1)S(1)}, u32[]{:S(2)}, u32[]{:S(2)}) collective-permute-start(bf16[1,64,640]{2,1,0:T(8,128)(2,1)S(1)} %slice.79), channel_id=1, source_target_pairs={{8,0},{16,8},{24,16},{9,1},{17,9},{25,17},{10,2},{18,10},{26,18},{... | collective-permute-start | bytes 245768 | tf_op jit(solution)/shard_map/ppermute | solution.py:10
  11.8 19.8 %collective-permute-start.2 = (bf16[11,64,640]{2,1,0:T(8,128)(2,1)S(1)}, bf16[11,64,640]{2,1,0:T(8,128)(2,1)}, u32[]{:S(2)}, u32[]{:S(2)}) collective-permute-start(bf16[11,64,640]{2,1,0:T(8,128)(2,1)S(1)} %constant_dynamic-update-slice_fusion), channel_id=1, source_target_pairs={{0,1},{1,2},{2,3},{3,4},{4,5},{5,6},{6,7},{7,0},{8,9},{9,10},{10,1... | collective-permute-start | bytes 2703368 | tf_op jit(solution)/shard_map/ppermute | solution.py:19
  14.3 22.3 %collective-permute-start.3 = (bf16[11,64,640]{2,1,0:T(8,128)(2,1)S(1)}, bf16[11,64,640]{2,1,0:T(8,128)(2,1)}, u32[]{:S(2)}, u32[]{:S(2)}) collective-permute-start(bf16[11,64,640]{2,1,0:T(8,128)(2,1)S(1)} %constant_dynamic-update-slice_fusion), channel_id=1, source_target_pairs={{1,0},{2,1},{3,2},{4,3},{5,4},{6,5},{7,6},{0,7},{9,8},{10,9},{11,1... | collective-permute-start | bytes 2703368 | tf_op jit(solution)/shard_map/ppermute | solution.py:22
  43.6 3.1 %copy-start.3 = (f32[640,9]{0,1:T(8,128)S(1)}, f32[640,9]{0,1:T(8,128)}, u32[]{:S(2)}) copy-start(f32[640,9]{0,1:T(8,128)} %bitcast_convert_fusion.1) | copy-start | bytes 69124
  64.1 7.9 %copy-start = (bf16[8,64,640]{2,1,0:T(8,128)(2,1)S(1)}, bf16[8,64,640]{2,1,0:T(8,128)(2,1)}, u32[]{:S(2)}) copy-start(bf16[8,64,640]{2,1,0:T(8,128)(2,1)} %param.7) | copy-start | bytes 1966084
  64.1 7.9 %copy-start.4 = (bf16[2,1280,640]{2,1,0:T(8,128)(2,1)S(1)}, bf16[2,1280,640]{2,1,0:T(8,128)(2,1)}, u32[]{:S(2)}) copy-start(bf16[2,1280,640]{2,1,0:T(8,128)(2,1)} %param.13) | copy-start | bytes 9830404
  72.0 14.5 %copy-start.2 = (bf16[1,9,640]{2,0,1:T(2,128)(2,1)S(1)}, bf16[1,9,640]{2,0,1:T(2,128)(2,1)}, u32[]{:S(2)}) copy-start(bf16[1,9,640]{2,0,1:T(2,128)(2,1)} %get-tuple-element.6) | copy-start | bytes 34564
  73.2 11.3 %collective-permute-start.4 = (bf16[2,64,640]{2,1,0:T(8,128)(2,1)S(1)}, bf16[2,64,640]{2,1,0:T(8,128)(2,1)S(1)}, u32[]{:S(2)}, u32[]{:S(2)}) collective-permute-start(bf16[2,64,640]{2,1,0:T(8,128)(2,1)S(1)} %slice.112), channel_id=1, source_target_pairs={{0,8},{8,16},{16,24},{1,9},{9,17},{17,25},{2,10},{10,18},{18,26},{... | collective-permute-start | bytes 491528 | tf_op jit(solution)/shard_map/ppermute | solution.py:10
  77.3 7.3 %collective-permute-start.5 = (bf16[1,64,640]{2,1,0:T(8,128)(2,1)S(1)}, bf16[1,64,640]{2,1,0:T(8,128)(2,1)S(1)}, u32[]{:S(2)}, u32[]{:S(2)}) collective-permute-start(bf16[1,64,640]{2,1,0:T(8,128)(2,1)S(1)} %slice.113), channel_id=1, source_target_pairs={{8,0},{16,8},{24,16},{9,1},{17,9},{25,17},{10,2},{18,10},{26,18},{... | collective-permute-start | bytes 245768 | tf_op jit(solution)/shard_map/ppermute | solution.py:10
  84.7 20.0 %collective-permute-start.6 = (bf16[11,64,640]{2,1,0:T(8,128)(2,1)S(1)}, bf16[11,64,640]{2,1,0:T(8,128)(2,1)S(1)}, u32[]{:S(2)}, u32[]{:S(2)}) collective-permute-start(bf16[11,64,640]{2,1,0:T(8,128)(2,1)S(1)} %pad_maximum_fusion.2), channel_id=1, source_target_pairs={{0,1},{1,2},{2,3},{3,4},{4,5},{5,6},{6,7},{7,0},{8,9},{9,10},{10,1... | collective-permute-start | bytes 2703368 | tf_op jit(solution)/shard_map/ppermute | solution.py:19
  86.5 21.3 %collective-permute-start.7 = (bf16[11,64,640]{2,1,0:T(8,128)(2,1)S(1)}, bf16[11,64,640]{2,1,0:T(8,128)(2,1)S(1)}, u32[]{:S(2)}, u32[]{:S(2)}) collective-permute-start(bf16[11,64,640]{2,1,0:T(8,128)(2,1)S(1)} %pad_maximum_fusion.2), channel_id=1, source_target_pairs={{1,0},{2,1},{3,2},{4,3},{5,4},{6,5},{7,6},{0,7},{9,8},{10,9},{11,1... | collective-permute-start | bytes 2703368 | tf_op jit(solution)/shard_map/ppermute | solution.py:22
  136.2 7.7 %copy-start.5 = (bf16[2,1280,640]{2,1,0:T(8,128)(2,1)S(1)}, bf16[2,1280,640]{2,1,0:T(8,128)(2,1)}, u32[]{:S(2)}) copy-start(bf16[2,1280,640]{2,1,0:T(8,128)(2,1)} %param.13) | copy-start | bytes 9830404
where the time goes:
time: 147 us; the launch traced here: 146 us
  matrix products  51.1 us (35%)
  waiting for transfers between devices  43.3 us (29%)
  local copies, waits for them, and re-layouts  21.4 us (15%)
  other arithmetic  15 us (10%)
  starting transfers between devices  14.9 us (10%)
    ppermute x2, waiting for transfers between devices, padded(): lax.ppermute(lax.slice_in_dim(block, block.shape[dim] - width, None, axis...  29.1 us
    dot_general x2, matrix products, shards(): jnp.einsum('akjrw,arwc->akjc', bands, stacked, preferred_element_type=jnp...  26.7 us
    unnamed x28, local copies, waits for them, and re-layouts  15.9 us
    dot_general x2, matrix products, channel_mlp(): jnp.dot(flat, first, preferred_element_type=jnp.float32)  15.6 us
    ppermute x4, starting transfers between devices, from_behind(): return lax.ppermute(block, axis, route)  10.5 us
    ppermute x2, waiting for transfers between devices, padded(): lax.ppermute(lax.slice_in_dim(block, 0, width, axis=dim), axis, backward)  8.24 us
    convert_element_type x2, other arithmetic, shards(): act = jax.nn.gelu(mixed, approximate=False).astype(jnp.bfloat16)  7.9 us
    ppermute x4, waiting for transfers between devices, from_behind(): return lax.ppermute(block, axis, route)  5.96 us
  transfers between devices with their start and end apart: 8, of which 5 were waited for; matrix products, arithmetic and copies ran while one was open for 8% of the time, Pallas kernels for 0%

commit v1 on v0

v1 whole, which is shorter than its diff:
```python
import functools

import jax
import jax.numpy as jnp
from jax import lax
from jax.experimental import pallas as pl
from jax.experimental.pallas import tpu as pltpu
from jax.sharding import PartitionSpec as P


F32 = jnp.float32
BF16 = jnp.bfloat16
ROWS = 4
STRIP = 16


def vmem():
    return pl.BlockSpec(memory_space=pltpu.VMEM)


def smem():
    return pl.BlockSpec(memory_space=pltpu.SMEM)


def gelu(x):
    return 0.5 * x * (1.0 + lax.erf(x * 0.7071067811865476))


def shift_table(reach):
    wide, strips = 4 * reach, reach // STRIP
    column = jnp.arange(3 * strips * 2 * reach, dtype=jnp.int32)
    section, strip = column // (strips * 2 * reach), column // (2 * reach) % strips
    lane = column % (2 * reach)
    tap = (section * reach - STRIP * strip + lane % reach) % wide
    source = lane // reach * wide + tap
    return (jnp.arange(2 * wide, dtype=jnp.int32)[:, None] == source[None, :]).astype(BF16)


def band_kernel(reach, parity, first, count, taps, table, band, rows, base):
    lats, filters, _, tap_count = taps.shape
    wide, strips = 4 * reach, reach // STRIP
    span = strips * 2 * reach
    order = [2 - parity[0], 0, 1 + parity[0]]
    rows[...] = jnp.zeros_like(rows)
    lane = lax.broadcasted_iota(jnp.int32, (ROWS, tap_count), 1) - reach

    def one(a, carry):
        inside = (lane >= first[a]) & (lane < first[a] + count[a])
        for k in range(filters):
            rows[k, 0:ROWS, 0:tap_count] = jnp.where(inside, taps[a, k].astype(F32), 0.0)
        for k in range(filters):
            for r in range(ROWS):
                skew = pltpu.roll(
                    jnp.broadcast_to(rows[k, r : r + 1, :], (STRIP, wide)),
                    0, 1, stride=1, stride_axis=0,
                )
                base[r // 2, k * STRIP : (k + 1) * STRIP, r % 2 * wide : (r % 2 + 1) * wide] = (
                    skew.astype(BF16)
                )
        for pair in range(ROWS // 2):
            for s in range(3):
                rolled = jnp.dot(
                    base[pair], table[:, s * span : (s + 1) * span], preferred_element_type=F32
                ).astype(BF16)
                for k in range(filters):
                    for b in range(strips):
                        row = k * reach + STRIP * b
                        band[
                            a,
                            order[s],
                            row : row + STRIP,
                            pair * 2 * reach : (pair + 1) * 2 * reach,
                        ] = rolled[k * STRIP : (k + 1) * STRIP, b * 2 * reach : (b + 1) * 2 * reach]
        return carry

    lax.fori_loop(0, lats, one, 0)


def make_bands(parity, first, count, taps, reach):
    lats, filters = taps.shape[:2]
    shape = (lats, 3, filters * reach, ROWS * reach)
    return pl.pallas_call(
        functools.partial(band_kernel, reach),
        out_shape=jax.ShapeDtypeStruct(shape, BF16),
        in_specs=[smem(), smem(), smem(), vmem(), vmem()],
        out_specs=vmem(),
        scratch_shapes=[
            pltpu.VMEM((filters, 8, 4 * reach), F32),
            pltpu.VMEM((ROWS // 2, filters * STRIP, 8 * reach), BF16),
        ],
        compiler_params=pltpu.CompilerParams(vmem_limit_bytes=10 << 20),
        cost_estimate=pl.CostEstimate(
            flops=4 << 30, bytes_accessed=lats * 3 << 20, transcendentals=0
        ),
        name="bands",
    )(parity, first, count, taps, shift_table(reach))


def mix_chunks(channels):
    step = 256
    return [(o, min(step, channels - o)) for o in range(0, channels, step)]


def convolve(bands, windows, conv, o, w):
    total = None
    for band, window in zip(bands, windows):
        part = jnp.dot(band, window[:, o : o + w], preferred_element_type=F32)
        total = part if total is None else total + part
    conv[:, o : o + w] = total


def mixed(conv, mix, reach, o, w):
    total = None
    for k in range(mix.shape[0]):
        part = conv[k * reach : (k + 1) * reach, o : o + w] * mix[k : k + 1, o : o + w].astype(F32)
        total = part if total is None else total + part
    return total


def extend(ext, above, own, below):
    lats = own.shape[0]
    ext[0:2] = above
    ext[2 : 2 + lats] = own
    ext[2 + lats : 3 + lats] = below


def pipelined(lats, fill, drain):
    def pair(i, carry):
        fill(2 * i, 0, jnp.maximum(2 * i - 1, 0), 1)
        fill(2 * i + 1, 1, 2 * i, 0)
        return carry

    lax.fori_loop(0, lats // 2, pair, 0)
    drain(lats - 1, 1)


def pre_kernel(
    layer, parity, first, count, band, own, above, below, near, near_halo, mixes, part,
    own_ext, near_ext, conv,
):
    lats, reach, channels = part.shape
    mix = mixes.at[layer]
    extend(own_ext, above[...], own[...], below[...])
    extend(near_ext, near_halo[0:2], near[...], near_halo[2:3])
    conv[1] = jnp.zeros_like(conv[1])

    def drain(a, slot, o=0, w=channels):
        part[a, :, o : o + w] = mixed(conv.at[slot], mix, reach, o, w)

    def fill(a, slot, last, other):
        def with_bands(exts):
            windows = [e[pl.ds(a, ROWS)].reshape(ROWS * reach, channels) for e in exts]
            bands = [band[a, s] for s in range(len(exts))]
            for o, w in mix_chunks(channels):
                convolve(bands, windows, conv.at[slot], o, w)
                drain(last, other, o, w)

        need = jnp.where(parity[0] == 0, (first[a] + count[a] > 1), (first[a] < 0))

        @pl.when(need)
        def _():
            with_bands([own_ext, near_ext])

        @pl.when(jnp.logical_not(need))
        def _():
            with_bands([own_ext])

    pipelined(lats, fill, drain)


def conv_near(layer, scalars, band, own, above, below, near, near_halo, mixes):
    lats, reach, channels = own.shape
    ext = pltpu.VMEM((lats + 3, reach, channels), BF16)
    return pl.pallas_call(
        functools.partial(pre_kernel, layer),
        out_shape=jax.ShapeDtypeStruct(own.shape, F32),
        in_specs=[smem()] * 3 + [vmem()] * 7,
        out_specs=vmem(),
        scratch_shapes=[ext, ext, pltpu.VMEM((2, band.shape[2], channels), F32)],
        compiler_params=pltpu.CompilerParams(vmem_limit_bytes=10 << 20),
        cost_estimate=pl.CostEstimate(
            flops=6 << 30, bytes_accessed=8 << 20, transcendentals=0
        ),
        name="conv_near",
    )(*scalars, band, own, above, below, near, near_halo, mixes)


def post_kernel(
    layer, band, far, far_halo, part, mixes, field, first, second, out,
    far_ext, conv, act, hidden,
):
    lats, reach, channels = part.shape
    mix = mixes.at[layer]
    extend(far_ext, far_halo[0:2], far[...], far_halo[2:3])
    conv[1] = jnp.zeros_like(conv[1])

    def drain(a, slot, o=0, w=channels):
        total = part[a, :, o : o + w] + mixed(conv.at[slot], mix, reach, o, w)
        act[pl.ds(pl.multiple_of(a * reach, reach), reach), o : o + w] = gelu(total).astype(BF16)

    def fill(a, slot, last, other):
        window = far_ext[pl.ds(a, ROWS)].reshape(ROWS * reach, channels)
        for o, w in mix_chunks(channels):
            convolve([band[a, 2]], [window], conv.at[slot], o, w)
            drain(last, other, o, w)

    pipelined(lats, fill, drain)
    for o, w in mix_chunks(first.shape[2]):
        up = jnp.dot(act[...], first[layer, :, o : o + w], preferred_element_type=F32)
        hidden[:, o : o + w] = gelu(up).astype(BF16)
    for o, w in mix_chunks(channels):
        update = jnp.dot(hidden[...], second[layer, :, o : o + w], preferred_element_type=F32)
        out[:, :, o : o + w] = (
            field[:, :, o : o + w].astype(F32) + update.reshape(lats, reach, w)
        ).astype(BF16)


def finish(layer, band, far, far_halo, part, mixes, field, first, second):
    lats, reach, channels = field.shape
    return pl.pallas_call(
        functools.partial(post_kernel, layer),
        out_shape=jax.ShapeDtypeStruct(field.shape, BF16),
        in_specs=[vmem()] * 8,
        out_specs=vmem(),
        scratch_shapes=[
            pltpu.VMEM((lats + 3, reach, channels), BF16),
            pltpu.VMEM((2, band.shape[2], channels), F32),
            pltpu.VMEM((lats * reach, channels), BF16),
            pltpu.VMEM((lats * reach, first.shape[2]), BF16),
        ],
        compiler_params=pltpu.CompilerParams(vmem_limit_bytes=14 << 20),
        cost_estimate=pl.CostEstimate(
            flops=5 << 30, bytes_accessed=8 << 20, transcendentals=1 << 20
        ),
        name="finish",
    )(band, far, far_halo, part, mixes, field, first, second)


def step_route(count, distance):
    return [(i, i + distance) for i in range(count) if 0 <= i + distance < count]


def shards(grid_state, filter_taps, support_start, support_count, filter_mix, w_in, w_out):
    reach = grid_state.shape[1]
    polar = lax.axis_size("polar")
    ring = lax.axis_size("azimuth")
    near_route = [(i, i ^ 1) for i in range(ring)]
    far_route = [(i, (i + 1 if i % 2 else i - 1) % ring) for i in range(ring)]
    parity = lax.rem(lax.axis_index("azimuth"), 2).reshape(1)
    scalars = (parity, support_start, support_count)
    band = make_bands(*scalars, filter_taps, reach)
    field = grid_state
    for layer in range(w_in.shape[0]):
        far = lax.ppermute(field, "azimuth", far_route)
        near = lax.ppermute(field, "azimuth", near_route)
        above = lax.ppermute(field[-2:], "polar", step_route(polar, 1))
        below = lax.ppermute(field[:1], "polar", step_route(polar, -1))
        halo = jnp.concatenate([above, below], axis=0)
        far_halo = lax.ppermute(halo, "azimuth", far_route)
        near_halo = lax.ppermute(halo, "azimuth", near_route)
        part = conv_near(
            layer, scalars, band, field, above, below, near, near_halo, filter_mix
        )
        field = finish(layer, band, far, far_halo, part, filter_mix, field, w_in, w_out)
    return field


def solution(mesh):
    return jax.shard_map(
        shards,
        mesh=mesh,
        in_specs=(
            P("polar", "azimuth", None),
            P("polar", None, None, None),
            P("polar"),
            P("polar"),
            P(),
            P(),
            P(),
        ),
        out_specs=P("polar", "azimuth", None),
        check_vma=False,
    )
```

time: 147 us -> 78.8 us (0.54)
  matrix products: 51.1 us -> 0 us
  Pallas kernels: 0 us -> 28.5 us
  local copies, waits for them, and re-layouts: 21.4 us -> 4.2 us
  waiting for transfers between devices: 43.3 us -> 26.8 us
  other arithmetic: 15 us -> 0.42 us
  starting transfers between devices: 14.9 us -> 18.4 us
    dot_general x7 -> x0, matrix products: 51.1 us -> none  [the longest x2 26.7 us: shards(): jnp.einsum('akjrw,arwc->akjc', bands, stacked, preferred_element_type=jnp...]
    pallas_call x0 -> x5, Pallas kernels: none -> 28.5 us  [the longest x2 11.6 us: conv_near(): pl.pallas_call(functools.partial(pre_kernel, layer), out_shape=jax.ShapeD...]
    ppermute x8 -> x12, waiting for transfers between devices: 43.3 us -> 26.8 us  [the longest x2 17.1 us: shards(): far_halo = lax.ppermute(halo, 'azimuth', far_route)]
    unnamed x28 -> x21, local copies, waits for them, and re-layouts: 15.9 us -> 2.28 us
    convert_element_type x2 -> x1, other arithmetic: 7.9 us -> 0.4 us  [shift_table(): (jnp.arange(2 * wide, dtype=jnp.int32)[:, None] == source[None, :]).astyp...]
    concatenate x3 -> x0, other arithmetic: 4.4 us -> none  [the longest x2 4.27 us: padded(): block = jnp.concatenate([low, block, high], axis=dim)]
    ppermute x8 -> x12, starting transfers between devices: 14.9 us -> 18.4 us  [the longest x2 7.02 us: shards(): above = lax.ppermute(field[-2:], 'polar', step_route(polar, 1))]
    another operation x2 -> x0, local copies, waits for them, and re-layouts: 2.07 us -> none  [shards(): stacked = jnp.stack([wide[lat_no:lat_no + 4] for lat_no in range(lat_rows)])]
  transfers between devices with their start and end apart: 8 -> 12, of which waited for: 5 -> 5; matrix products, arithmetic and copies ran while one was open for 8% -> 3% of each run, Pallas kernels for 0% -> 23%
where the time goes in v1:
time: 78.8 us; the launch traced here: 78.5 us
  Pallas kernels  28.5 us (36%)
  waiting for transfers between devices  26.8 us (34%)
  starting transfers between devices  18.4 us (23%)
  local copies, waits for them, and re-layouts  4.2 us (5%)
    ppermute x2, waiting for transfers between devices, shards(): far_halo = lax.ppermute(halo, 'azimuth', far_route)  17.1 us
    pallas_call x2, Pallas kernels, conv_near(): pl.pallas_call(functools.partial(pre_kernel, layer), out_shape=jax.ShapeD...  11.6 us
    pallas_call x2, Pallas kernels, finish(): pl.pallas_call(functools.partial(post_kernel, layer), out_shape=jax.Shape...  10.8 us
    ppermute x2, waiting for transfers between devices, shards(): below = lax.ppermute(field[:1], 'polar', step_route(polar, -1))  7.5 us
    ppermute x2, starting transfers between devices, shards(): above = lax.ppermute(field[-2:], 'polar', step_route(polar, 1))  7.02 us
    pallas_call x1, Pallas kernels, make_bands(): pl.pallas_call(functools.partial(band_kernel, reach), out_shape=jax.Shape...  6.09 us
    ppermute x2, starting transfers between devices, shards(): near_halo = lax.ppermute(halo, 'azimuth', near_route)  3.74 us
    ppermute x2, starting transfers between devices, shards(): far = lax.ppermute(field, 'azimuth', far_route)  2.66 us
  transfers between devices with their start and end apart: 12, of which 5 were waited for; matrix products, arithmetic and copies ran while one was open for 3% of the time, Pallas kernels for 23%

profile of v1, /device:TPU:1, one launch (start us, length us, event | category | flops | bytes accessed | tf_op | source)
XLA Modules:
  0.0 78.5 jit_solution(6989457891778737226)
XLA Ops:
  0.0 0.0 collective-permute-start.4
  0.0 2.7 %collective-permute-start = (bf16[8,64,640]{2,1,0:T(8,128)(2,1)}, bf16[8,64,640]{2,1,0:T(8,128)(2,1)S(1)}, u32[]{:S(2)}, u32[]{:S(2)}) collective-permute-start(bf16[8,64,640]{2,1,0:T(8,128)(2,1)} %field.1), channel_id=1, source_target_pairs={{0,7},{1,2},{2,1},{3,4},{4,3},{5,6},{6,5},{7,0},{8,15},{9,10},{10,... | collective-permute-start | bytes 1966088 | tf_op jit(solution)/shard_map/ppermute | solution.py:254
  2.7 1.0 %slice.12 = bf16[2,64,640]{2,1,0:T(8,128)(2,1)S(1)} slice(bf16[8,64,640]{2,1,0:T(8,128)(2,1)} %field.1), slice={[6:8], [0:64], [0:640]} | slice | bytes 327680 | tf_op jit(solution)/shard_map/slice | solution.py:256
  3.6 3.1 %collective-permute-start.1 = (bf16[2,64,640]{2,1,0:T(8,128)(2,1)S(1)}, bf16[2,64,640]{2,1,0:T(8,128)(2,1)S(1)}, u32[]{:S(2)}, u32[]{:S(2)}) collective-permute-start(bf16[2,64,640]{2,1,0:T(8,128)(2,1)S(1)} %slice.12), channel_id=1, source_target_pairs={{0,8},{8,16},{16,24},{1,9},{9,17},{17,25},{2,10},{10,18},{18,26},{... | collective-permute-start | bytes 491528 | tf_op jit(solution)/shard_map/ppermute | solution.py:256
  6.8 0.9 %slice.13 = bf16[1,64,640]{2,1,0:T(8,128)(2,1)S(1)} slice(bf16[8,64,640]{2,1,0:T(8,128)(2,1)} %field.1), slice={[0:1], [0:64], [0:640]} | slice | bytes 163840 | tf_op jit(solution)/shard_map/slice | solution.py:257
  7.7 1.3 %collective-permute-start.2 = (bf16[1,64,640]{2,1,0:T(8,128)(2,1)S(1)}, bf16[1,64,640]{2,1,0:T(8,128)(2,1)S(1)}, u32[]{:S(2)}, u32[]{:S(2)}) collective-permute-start(bf16[1,64,640]{2,1,0:T(8,128)(2,1)S(1)} %slice.13), channel_id=1, source_target_pairs={{8,0},{16,8},{24,16},{9,1},{17,9},{25,17},{10,2},{18,10},{26,18},{... | collective-permute-start | bytes 245768 | tf_op jit(solution)/shard_map/ppermute | solution.py:257
  9.0 0.4 fusion.table
  9.4 0.0 collective-permute-done.1.above
  9.4 4.6 %collective-permute-done.2.below = bf16[1,64,640]{2,1,0:T(8,128)(2,1)S(1)} collective-permute-done((bf16[1,64,640]{2,1,0:T(8,128)(2,1)S(1)}, bf16[1,64,640]{2,1,0:T(8,128)(2,1)S(1)}, u32[]{:S(2)}, u32[]{:S(2)}) %collective-permute-start.2) | collective-permute-done | bytes 81952 | tf_op jit(solution)/shard_map/ppermute | solution.py:257
  14.0 2.9 %collective-permute-start.5 = (bf16[3,64,640]{2,1,0:T(8,128)(2,1)S(1)}, bf16[3,64,640]{2,1,0:T(8,128)(2,1)S(1)}, u32[]{:S(2)}, u32[]{:S(2)}) collective-permute-start(bf16[3,64,640]{2,1,0:T(8,128)(2,1)S(1)} %constant_dynamic-update-slice_fusion), channel_id=1, source_target_pairs={{0,1},{1,0},{2,3},{3,2},{4,5},{5,4},{6,7},{7,6},{8,9},{9,8},{10,11... | collective-permute-start | bytes 737288 | tf_op jit(solution)/shard_map/ppermute | solution.py:260
  16.9 0.0 copy-start.3
  16.9 0.9 %copy-done.3 = bf16[8,9,4,129]{3,2,1,0:T(4,128)(2,1)S(1)} copy-done((bf16[8,9,4,129]{3,2,1,0:T(4,128)(2,1)S(1)}, bf16[8,9,4,129]{3,2,1,0:T(4,128)(2,1)}, u32[]{:S(2)}) %copy-start.3) | copy-done | bytes 74328
  17.8 0.0 copy-start.4
  17.8 0.7 copy-done.4
  18.5 0.0 copy-start.6
  18.5 0.7 copy-done.6
  19.1 0.0 copy-start.8
  19.1 0.0 copy-start
  19.1 0.0 copy-start.5
  19.1 0.0 copy-start.7
  19.1 6.1 %bands.1.band = bf16[8,3,576,256]{3,2,1,0:T(8,128)(2,1)S(1)} custom-call(s32[1]{0:T(128)} %bitcast.parity, s32[8]{0:T(128)S(1)} %copy-done.4, s32[8]{0:T(128)S(1)} %copy-done.6, bf16[8,9,4,129]{3,2,1,0:T(4,128)(2,1)S(1)} %copy-done.3, bf16[512,1536]{1,0:T(8,128)(2,1)S(1)} %fusion.table), custom_call_target="tpu_custom_call" | custom-call | flops 4294967296 | bytes 25165824 | tf_op jit(solution)/shard_map/bands/pallas_call | solution.py:82
  25.2 0.0 copy-done.8
  25.2 0.0 copy-start.1
  25.3 0.0 copy-start.2
  25.3 0.1 collective-permute-start.3
  25.3 0.0 collective-permute-done.5.near_halo
  25.4 0.0 collective-permute-done.4.near
  25.4 0.0 copy-done
  25.4 0.0 copy-done.5
  25.4 0.0 copy-done.7
  25.4 5.8 %conv_near.2.part = f32[8,64,640]{2,1,0:T(8,128)S(1)} custom-call(s32[1]{0:T(128)} %bitcast.parity, s32[8]{0:T(128)S(1)} %copy-done.5, s32[8]{0:T(128)S(1)} %copy-done.7, bf16[8,3,576,256]{3,2,1,0:T(8,128)(2,1)S(1)} %bands.1.band, bf16[8,64,640]{2,1,0:T(8,128)(2,1)S(1)} %copy-done, bf16[2,64,640]{2,1,0:T(8,128)(2,1)S(1)} %collective-permute-done.1.above, ...), custom_call_target="tpu_custom_call" | custom-call | flops 6442450944 | bytes 8388608 | tf_op jit(solution)/shard_map/conv_near/pallas_call | solution.py:174
  31.2 2.4 %collective-permute-done.3.far_halo = bf16[3,64,640]{2,1,0:T(8,128)(2,1)S(1)} collective-permute-done((bf16[3,64,640]{2,1,0:T(8,128)(2,1)S(1)}, bf16[3,64,640]{2,1,0:T(8,128)(2,1)S(1)}, u32[]{:S(2)}, u32[]{:S(2)}) %collective-permute-start.3) | collective-permute-done | bytes 245792 | tf_op jit(solution)/shard_map/ppermute | solution.py:259
  33.6 0.0 collective-permute-done.far
  33.6 0.0 copy-done.1
  33.6 0.0 copy-done.2
  33.6 5.0 %finish.2.own.field = bf16[8,64,640]{2,1,0:T(8,128)(2,1)S(1)} custom-call(bf16[8,3,576,256]{3,2,1,0:T(8,128)(2,1)S(1)} %bands.1.band, bf16[8,64,640]{2,1,0:T(8,128)(2,1)S(1)} %collective-permute-done.far, bf16[3,64,640]{2,1,0:T(8,128)(2,1)S(1)} %collective-permute-done.3.far_halo, f32[8,64,640]{2,1,0:T(8,128)S(1)} %conv_near.2.part, ...), custom_call_target="tpu_custom_call" | custom-call | flops 5368709120 | bytes 8388608 | tf_op jit(solution)/shard_map/finish/pallas_call | solution.py:220
  38.7 0.6 collective-permute-start.10
  39.2 3.9 %collective-permute-start.7 = (bf16[2,64,640]{2,1,0:T(8,128)(2,1)S(1)}, bf16[2,64,640]{2,1,0:T(8,128)(2,1)S(1)}, u32[]{:S(2)}, u32[]{:S(2)}) collective-permute-start(bf16[2,64,640]{2,1,0:T(8,128)(2,1)S(1)} %slice.16), channel_id=1, source_target_pairs={{0,8},{8,16},{16,24},{1,9},{9,17},{17,25},{2,10},{10,18},{18,26},{... | collective-permute-start | bytes 491528 | tf_op jit(solution)/shard_map/ppermute | solution.py:256
  43.2 1.3 %collective-permute-start.8 = (bf16[1,64,640]{2,1,0:T(8,128)(2,1)S(1)}, bf16[1,64,640]{2,1,0:T(8,128)(2,1)S(1)}, u32[]{:S(2)}, u32[]{:S(2)}) collective-permute-start(bf16[1,64,640]{2,1,0:T(8,128)(2,1)S(1)} %slice.17), channel_id=1, source_target_pairs={{8,0},{16,8},{24,16},{9,1},{17,9},{25,17},{10,2},{18,10},{26,18},{... | collective-permute-start | bytes 245768 | tf_op jit(solution)/shard_map/ppermute | solution.py:257
  44.5 2.1 %collective-permute-done.7.above = bf16[2,64,640]{2,1,0:T(8,128)(2,1)S(1)} collective-permute-done((bf16[2,64,640]{2,1,0:T(8,128)(2,1)S(1)}, bf16[2,64,640]{2,1,0:T(8,128)(2,1)S(1)}, u32[]{:S(2)}, u32[]{:S(2)}) %collective-permute-start.7) | collective-permute-done | bytes 163872 | tf_op jit(solution)/shard_map/ppermute | solution.py:256
  46.6 2.9 %collective-permute-done.8.below = bf16[1,64,640]{2,1,0:T(8,128)(2,1)S(1)} collective-permute-done((bf16[1,64,640]{2,1,0:T(8,128)(2,1)S(1)}, bf16[1,64,640]{2,1,0:T(8,128)(2,1)S(1)}, u32[]{:S(2)}, u32[]{:S(2)}) %collective-permute-start.8) | collective-permute-done | bytes 81952 | tf_op jit(solution)/shard_map/ppermute | solution.py:257
  49.5 0.9 %collective-permute-start.11 = (bf16[3,64,640]{2,1,0:T(8,128)(2,1)S(1)}, bf16[3,64,640]{2,1,0:T(8,128)(2,1)S(1)}, u32[]{:S(2)}, u32[]{:S(2)}) collective-permute-start(bf16[3,64,640]{2,1,0:T(8,128)(2,1)S(1)} %constant_dynamic-update-slice_fusion.2), channel_id=1, source_target_pairs={{0,1},{1,0},{2,3},{3,2},{4,5},{5,4},{6,7},{7,6},{8,9},{9,8},{10,11... | collective-permute-start | bytes 737288 | tf_op jit(solution)/shard_map/ppermute | solution.py:260
  50.4 0.0 collective-permute-start.6
  50.4 1.7 %collective-permute-start.9 = (bf16[3,64,640]{2,1,0:T(8,128)(2,1)S(1)}, bf16[3,64,640]{2,1,0:T(8,128)(2,1)S(1)}, u32[]{:S(2)}, u32[]{:S(2)}) collective-permute-start(bf16[3,64,640]{2,1,0:T(8,128)(2,1)S(1)} %constant_dynamic-update-slice_fusion.2), channel_id=1, source_target_pairs={{0,7},{1,2},{2,1},{3,4},{4,3},{5,6},{6,5},{7,0},{8,15},{9,10},{10,... | collective-permute-start | bytes 737288 | tf_op jit(solution)/shard_map/ppermute | solution.py:259
  52.2 0.0 collective-permute-done.11.near_halo
  52.2 0.0 collective-permute-done.10.near
  52.2 5.8 %conv_near.3.part = f32[8,64,640]{2,1,0:T(8,128)S(1)} custom-call(s32[1]{0:T(128)} %bitcast.parity, s32[8]{0:T(128)S(1)} %copy-done.5, s32[8]{0:T(128)S(1)} %copy-done.7, bf16[8,3,576,256]{3,2,1,0:T(8,128)(2,1)S(1)} %bands.1.band, bf16[8,64,640]{2,1,0:T(8,128)(2,1)S(1)} %finish.2.own.field, bf16[2,64,640]{2,1,0:T(8,128)(2,1)S(1)} %collective-permute-done.7.above, ...), custom_call_target="tpu_custom_call" | custom-call | flops 6442450944 | bytes 8388608 | tf_op jit(solution)/shard_map/conv_near/pallas_call | solution.py:174
  58.0 14.7 %collective-permute-done.9.far_halo = bf16[3,64,640]{2,1,0:T(8,128)(2,1)S(1)} collective-permute-done((bf16[3,64,640]{2,1,0:T(8,128)(2,1)S(1)}, bf16[3,64,640]{2,1,0:T(8,128)(2,1)S(1)}, u32[]{:S(2)}, u32[]{:S(2)}) %collective-permute-start.9) | collective-permute-done | bytes 245792 | tf_op jit(solution)/shard_map/ppermute | solution.py:259
  72.7 0.0 collective-permute-done.6.far
  72.7 5.8 %finish.3 = bf16[8,64,640]{2,1,0:T(8,128)(2,1)} custom-call(bf16[8,3,576,256]{3,2,1,0:T(8,128)(2,1)S(1)} %bands.1.band, bf16[8,64,640]{2,1,0:T(8,128)(2,1)S(1)} %collective-permute-done.6.far, bf16[3,64,640]{2,1,0:T(8,128)(2,1)S(1)} %collective-permute-done.9.far_halo, f32[8,64,640]{2,1,0:T(8,128)S(1)} %conv_near.3.part, bf16[2,9,640]{2,1,0:T(8,128)(2,1)S(1)} %copy.8.mixes, ...), custom_call_target="tpu_custom_call" | custom-call | flops 5368709120 | bytes 8388608 | tf_op jit(solution)/shard_map/finish/pallas_call | solution.py:220
  (8 shorter events, 0.1 us)
Async XLA Ops:
  0.0 25.4 %collective-permute-start.4 = (bf16[8,64,640]{2,1,0:T(8,128)(2,1)}, bf16[8,64,640]{2,1,0:T(8,128)(2,1)S(1)}, u32[]{:S(2)}, u32[]{:S(2)}) collective-permute-start(bf16[8,64,640]{2,1,0:T(8,128)(2,1)} %field.1), channel_id=1, source_target_pairs={{0,1},{1,0},{2,3},{3,2},{4,5},{5,4},{6,7},{7,6},{8,9},{9,8},{10,11... | collective-permute-start | bytes 1966088 | tf_op jit(solution)/shard_map/ppermute | solution.py:255
  0.0 33.6 %collective-permute-start = (bf16[8,64,640]{2,1,0:T(8,128)(2,1)}, bf16[8,64,640]{2,1,0:T(8,128)(2,1)S(1)}, u32[]{:S(2)}, u32[]{:S(2)}) collective-permute-start(bf16[8,64,640]{2,1,0:T(8,128)(2,1)} %field.1), channel_id=1, source_target_pairs={{0,7},{1,2},{2,1},{3,4},{4,3},{5,6},{6,5},{7,0},{8,15},{9,10},{10,... | collective-permute-start | bytes 1966088 | tf_op jit(solution)/shard_map/ppermute | solution.py:254
  3.6 5.8 %collective-permute-start.1 = (bf16[2,64,640]{2,1,0:T(8,128)(2,1)S(1)}, bf16[2,64,640]{2,1,0:T(8,128)(2,1)S(1)}, u32[]{:S(2)}, u32[]{:S(2)}) collective-permute-start(bf16[2,64,640]{2,1,0:T(8,128)(2,1)S(1)} %slice.12), channel_id=1, source_target_pairs={{0,8},{8,16},{16,24},{1,9},{9,17},{17,25},{2,10},{10,18},{18,26},{... | collective-permute-start | bytes 491528 | tf_op jit(solution)/shard_map/ppermute | solution.py:256
  7.7 6.3 %collective-permute-start.2 = (bf16[1,64,640]{2,1,0:T(8,128)(2,1)S(1)}, bf16[1,64,640]{2,1,0:T(8,128)(2,1)S(1)}, u32[]{:S(2)}, u32[]{:S(2)}) collective-permute-start(bf16[1,64,640]{2,1,0:T(8,128)(2,1)S(1)} %slice.13), channel_id=1, source_target_pairs={{8,0},{16,8},{24,16},{9,1},{17,9},{25,17},{10,2},{18,10},{26,18},{... | collective-permute-start | bytes 245768 | tf_op jit(solution)/shard_map/ppermute | solution.py:257
  14.0 11.3 %collective-permute-start.5 = (bf16[3,64,640]{2,1,0:T(8,128)(2,1)S(1)}, bf16[3,64,640]{2,1,0:T(8,128)(2,1)S(1)}, u32[]{:S(2)}, u32[]{:S(2)}) collective-permute-start(bf16[3,64,640]{2,1,0:T(8,128)(2,1)S(1)} %constant_dynamic-update-slice_fusion), channel_id=1, source_target_pairs={{0,1},{1,0},{2,3},{3,2},{4,5},{5,4},{6,7},{7,6},{8,9},{9,8},{10,11... | collective-permute-start | bytes 737288 | tf_op jit(solution)/shard_map/ppermute | solution.py:260
  16.9 0.9 %copy-start.3 = (bf16[8,9,4,129]{3,2,1,0:T(4,128)(2,1)S(1)}, bf16[8,9,4,129]{3,2,1,0:T(4,128)(2,1)}, u32[]{:S(2)}) copy-start(bf16[8,9,4,129]{3,2,1,0:T(4,128)(2,1)} %taps.1) | copy-start | bytes 222916
  17.8 0.7 copy-start.4
  18.5 0.7 copy-start.6
  19.1 6.1 %copy-start.8 = (bf16[2,9,640]{2,0,1:T(2,128)(2,1)S(1)}, bf16[2,9,640]{2,0,1:T(2,128)(2,1)}, u32[]{:S(2)}) copy-start(bf16[2,9,640]{2,0,1:T(2,128)(2,1)} %param.11) | copy-start | bytes 69124
  19.1 6.3 %copy-start = (bf16[8,64,640]{2,1,0:T(8,128)(2,1)S(1)}, bf16[8,64,640]{2,1,0:T(8,128)(2,1)}, u32[]{:S(2)}) copy-start(bf16[8,64,640]{2,1,0:T(8,128)(2,1)} %field.1) | copy-start | bytes 1966084
  19.1 6.3 %copy-start.5 = (s32[8]{0:T(128)S(1)}, s32[8]{0:T(128)}, u32[]{:S(2)}) copy-start(s32[8]{0:T(128)} %first.8) | copy-start | bytes 100
  19.1 6.3 %copy-start.7 = (s32[8]{0:T(128)S(1)}, s32[8]{0:T(128)}, u32[]{:S(2)}) copy-start(s32[8]{0:T(128)} %count.5) | copy-start | bytes 100
  25.2 8.4 %copy-start.1 = (bf16[2,640,1280]{2,1,0:T(8,128)(2,1)S(1)}, bf16[2,640,1280]{2,1,0:T(8,128)(2,1)}, u32[]{:S(2)}) copy-start(bf16[2,640,1280]{2,1,0:T(8,128)(2,1)} %first.9) | copy-start | bytes 9830404
  25.3 8.4 %copy-start.2 = (bf16[2,1280,640]{2,1,0:T(8,128)(2,1)S(1)}, bf16[2,1280,640]{2,1,0:T(8,128)(2,1)}, u32[]{:S(2)}) copy-start(bf16[2,1280,640]{2,1,0:T(8,128)(2,1)} %second.3) | copy-start | bytes 9830404
  25.3 8.4 %collective-permute-start.3 = (bf16[3,64,640]{2,1,0:T(8,128)(2,1)S(1)}, bf16[3,64,640]{2,1,0:T(8,128)(2,1)S(1)}, u32[]{:S(2)}, u32[]{:S(2)}) collective-permute-start(bf16[3,64,640]{2,1,0:T(8,128)(2,1)S(1)} %constant_dynamic-update-slice_fusion), channel_id=1, source_target_pairs={{0,7},{1,2},{2,1},{3,4},{4,3},{5,6},{6,5},{7,0},{8,15},{9,10},{10,... | collective-permute-start | bytes 737288 | tf_op jit(solution)/shard_map/ppermute | solution.py:259
  38.7 13.5 %collective-permute-start.10 = (bf16[8,64,640]{2,1,0:T(8,128)(2,1)S(1)}, bf16[8,64,640]{2,1,0:T(8,128)(2,1)S(1)}, u32[]{:S(2)}, u32[]{:S(2)}) collective-permute-start(bf16[8,64,640]{2,1,0:T(8,128)(2,1)S(1)} %finish.2.own.field), channel_id=1, source_target_pairs={{0,1},{1,0},{2,3},{3,2},{4,5},{5,4},{6,7},{7,6},{8,9},{9,8},{10,11... | collective-permute-start | bytes 1966088 | tf_op jit(solution)/shard_map/ppermute | solution.py:255
  39.2 7.3 %collective-permute-start.7 = (bf16[2,64,640]{2,1,0:T(8,128)(2,1)S(1)}, bf16[2,64,640]{2,1,0:T(8,128)(2,1)S(1)}, u32[]{:S(2)}, u32[]{:S(2)}) collective-permute-start(bf16[2,64,640]{2,1,0:T(8,128)(2,1)S(1)} %slice.16), channel_id=1, source_target_pairs={{0,8},{8,16},{16,24},{1,9},{9,17},{17,25},{2,10},{10,18},{18,26},{... | collective-permute-start | bytes 491528 | tf_op jit(solution)/shard_map/ppermute | solution.py:256
  43.2 6.4 %collective-permute-start.8 = (bf16[1,64,640]{2,1,0:T(8,128)(2,1)S(1)}, bf16[1,64,640]{2,1,0:T(8,128)(2,1)S(1)}, u32[]{:S(2)}, u32[]{:S(2)}) collective-permute-start(bf16[1,64,640]{2,1,0:T(8,128)(2,1)S(1)} %slice.17), channel_id=1, source_target_pairs={{8,0},{16,8},{24,16},{9,1},{17,9},{25,17},{10,2},{18,10},{26,18},{... | collective-permute-start | bytes 245768 | tf_op jit(solution)/shard_map/ppermute | solution.py:257
  49.5 2.6 %collective-permute-start.11 = (bf16[3,64,640]{2,1,0:T(8,128)(2,1)S(1)}, bf16[3,64,640]{2,1,0:T(8,128)(2,1)S(1)}, u32[]{:S(2)}, u32[]{:S(2)}) collective-permute-start(bf16[3,64,640]{2,1,0:T(8,128)(2,1)S(1)} %constant_dynamic-update-slice_fusion.2), channel_id=1, source_target_pairs={{0,1},{1,0},{2,3},{3,2},{4,5},{5,4},{6,7},{7,6},{8,9},{9,8},{10,11... | collective-permute-start | bytes 737288 | tf_op jit(solution)/shard_map/ppermute | solution.py:260
  50.4 22.3 %collective-permute-start.6 = (bf16[8,64,640]{2,1,0:T(8,128)(2,1)S(1)}, bf16[8,64,640]{2,1,0:T(8,128)(2,1)S(1)}, u32[]{:S(2)}, u32[]{:S(2)}) collective-permute-start(bf16[8,64,640]{2,1,0:T(8,128)(2,1)S(1)} %finish.2.own.field), channel_id=1, source_target_pairs={{0,7},{1,2},{2,1},{3,4},{4,3},{5,6},{6,5},{7,0},{8,15},{9,10},{10,... | collective-permute-start | bytes 1966088 | tf_op jit(solution)/shard_map/ppermute | solution.py:254
  50.4 22.3 %collective-permute-start.9 = (bf16[3,64,640]{2,1,0:T(8,128)(2,1)S(1)}, bf16[3,64,640]{2,1,0:T(8,128)(2,1)S(1)}, u32[]{:S(2)}, u32[]{:S(2)}) collective-permute-start(bf16[3,64,640]{2,1,0:T(8,128)(2,1)S(1)} %constant_dynamic-update-slice_fusion.2), channel_id=1, source_target_pairs={{0,7},{1,2},{2,1},{3,4},{4,3},{5,6},{6,5},{7,0},{8,15},{9,10},{10,... | collective-permute-start | bytes 737288 | tf_op jit(solution)/shard_map/ppermute | solution.py:259

commit v2 on v1

v2 whole, which is shorter than its diff:
```python
import functools

import jax
import jax.numpy as jnp
from jax import lax
from jax.experimental import pallas as pl
from jax.experimental.pallas import tpu as pltpu
from jax.sharding import PartitionSpec as P


F32 = jnp.float32
BF16 = jnp.bfloat16
ROWS = 4
STRIP = 16


def vmem():
    return pl.BlockSpec(memory_space=pltpu.VMEM)


def smem():
    return pl.BlockSpec(memory_space=pltpu.SMEM)


def gelu(x):
    return 0.5 * x * (1.0 + lax.erf(x * 0.7071067811865476))


def shift_tables(reach):
    wide, strips = 4 * reach, reach // STRIP
    column = jnp.arange(3 * strips * reach, dtype=jnp.int32)[None, :]
    odd = jnp.arange(2, dtype=jnp.int32)[:, None]
    section, strip = column // (strips * reach), column // reach % strips
    strip = strip + odd * (1 - 2 * (strip % 2))
    tap = (section * reach - STRIP * strip + column % reach) % wide
    return (jnp.arange(wide, dtype=jnp.int32)[None, :, None] == tap[:, None, :]).astype(BF16)


def band_kernel(reach, info, taps, table, band, rows, base):
    lats, filters, _, tap_count = taps.shape
    wide, strips = 4 * reach, reach // STRIP
    parity = info[2 * lats]
    order = [2 - parity, 0, 1 + parity]
    block = filters * STRIP
    rows[...] = jnp.zeros_like(rows)
    lane = lax.broadcasted_iota(jnp.int32, (ROWS, tap_count), 1) - reach

    def skewed(a, carry):
        inside = (lane >= info[a]) & (lane < info[a] + info[lats + a])
        for k in range(filters):
            rows[k, 0:ROWS, 0:tap_count] = jnp.where(inside, taps[a, k].astype(F32), 0.0)
        for k in range(filters):
            at = pl.ds(pl.multiple_of(a * block + k * STRIP, STRIP), STRIP)
            for r in range(ROWS):
                skew = pltpu.roll(
                    jnp.broadcast_to(rows[k, r : r + 1, :], (STRIP, wide)),
                    0, 1, stride=1, stride_axis=0,
                )
                base[r, at, :] = skew.astype(BF16)
        return carry

    lax.fori_loop(0, lats, skewed, 0)
    low = lax.broadcasted_iota(jnp.int32, (lats * block, 2 * reach), 1) < reach
    for s in range(3):
        columns = slice(s * strips * reach, (s + 1) * strips * reach)
        for pair in range(ROWS // 2):
            even, odd = (
                jnp.dot(base[2 * pair + m], table[m, :, columns], preferred_element_type=F32).astype(BF16)
                for m in range(2)
            )
            for b in range(0, strips, 2):
                e, o = (x[:, b * reach : (b + 2) * reach] for x in (even, odd))
                joined = [jnp.where(low, e, o), pltpu.roll(jnp.where(low, o, e), reach, 1)]
                for c in range(2):
                    for a in range(lats):
                        for k in range(filters):
                            at = k * reach + STRIP * (b + c)
                            row = a * block + k * STRIP
                            band[
                                a,
                                order[s],
                                at : at + STRIP,
                                pair * 2 * reach : (pair + 1) * 2 * reach,
                            ] = joined[c][row : row + STRIP]


def make_bands(info, taps, reach):
    lats, filters = taps.shape[:2]
    shape = (lats, 3, filters * reach, ROWS * reach)
    return pl.pallas_call(
        functools.partial(band_kernel, reach),
        out_shape=jax.ShapeDtypeStruct(shape, BF16),
        in_specs=[smem(), vmem(), vmem()],
        out_specs=vmem(),
        scratch_shapes=[
            pltpu.VMEM((filters, 8, 4 * reach), F32),
            pltpu.VMEM((ROWS, lats * filters * STRIP, 4 * reach), BF16),
        ],
        compiler_params=pltpu.CompilerParams(vmem_limit_bytes=12 << 20),
        cost_estimate=pl.CostEstimate(
            flops=4 << 30, bytes_accessed=lats * 3 << 20, transcendentals=0
        ),
        name="bands",
    )(info, taps, shift_tables(reach))


def split_rows(rows, down, up, edge, body):
    lats = rows.shape[0]
    top, rest, end = pl.ds(0, 1), pl.ds(1, lats - 3), pl.ds(lats - 2, 2)
    return [
        (rows.at[end], down),
        (rows.at[top], up),
        (rows.at[end], edge.at[pl.ds(0, 2)]),
        (rows.at[top], edge.at[pl.ds(2, 1)]),
        (rows.at[rest], body),
    ]


def fetch_kernel(field, taps, down, up, edge, body, taps_out, sem):
    moves = split_rows(field, down, up, edge, body) + [(taps, taps_out)]
    moves = [pltpu.make_async_copy(s, d, sem.at[i]) for i, (s, d) in enumerate(moves)]
    for m in moves:
        m.start()
    for m in moves:
        m.wait()


def fetch(field, taps):
    shapes = [(n,) + field.shape[1:] for n in (2, 1, 3, field.shape[0] - 3)] + [taps.shape]
    return pl.pallas_call(
        fetch_kernel,
        out_shape=[jax.ShapeDtypeStruct(s, BF16) for s in shapes],
        in_specs=[pl.BlockSpec(memory_space=pl.ANY)] * 2,
        out_specs=[vmem()] * len(shapes),
        scratch_shapes=[pltpu.SemaphoreType.DMA((6,))],
        compiler_params=pltpu.CompilerParams(vmem_limit_bytes=60 << 20),
        cost_estimate=pl.CostEstimate(flops=0, bytes_accessed=1 << 20, transcendentals=0),
        name="fetch",
    )(field, taps)


def mix_chunks(channels):
    step = 256
    return [(o, min(step, channels - o)) for o in range(0, channels, step)]


def convolve(bands, windows, conv, o, w):
    total = None
    for band, window in zip(bands, windows):
        part = jnp.dot(band, window[:, o : o + w], preferred_element_type=F32)
        total = part if total is None else total + part
    conv[:, o : o + w] = total


def mixed(conv, mixes, layer, reach, o, w):
    total = None
    for k in range(mixes.shape[0]):
        mix = mixes[k, layer : layer + 1, o : o + w].astype(F32)
        part = conv[k * reach : (k + 1) * reach, o : o + w] * mix
        total = part if total is None else total + part
    return total


def local_kernel(layer, inner, info, band, *refs):
    if inner:
        own, near, mixes, part, conv = refs
        halos = (None, None)
    else:
        own, own_halo, near, near_halo, mixes, part, conv = refs
        halos = (own_halo, near_halo)
    lats, reach, channels = own.shape

    def drain(p, slot, o=0, w=channels):
        part[p, :, o : o + w] = mixed(conv.at[slot], mixes, layer, reach, o, w)

    def fill(a, slot, last):
        def window(block, halo):
            if inner:
                rows = block[pl.ds(a - 2, ROWS)]
            elif a < 2:
                rows = jnp.concatenate([halo[a:2], block[0 : a + 2]], axis=0)
            else:
                rows = jnp.concatenate([block[a - 2 : lats], halo[2:3]], axis=0)
            return rows.reshape(ROWS * reach, channels)

        def with_sections(blocks):
            windows = [window(b, h) for b, h in zip(blocks, halos)]
            bands = [band[a, s] for s in range(len(blocks))]
            for o, w in mix_chunks(channels):
                convolve(bands, windows, conv.at[slot], o, w)
                if last is not None:
                    drain(last, 1 - slot, o, w)

        need = jnp.where(info[2 * lats] == 0, info[a] + info[lats + a] > 1, info[a] < 0)

        @pl.when(need)
        def _():
            with_sections([own, near])

        @pl.when(jnp.logical_not(need))
        def _():
            with_sections([own])

    count = part.shape[0]
    if inner:
        looped = count // 2 * 2

        def pair(i, carry):
            fill(2 * i + 2, 0, jnp.maximum(2 * i - 1, 0))
            fill(2 * i + 3, 1, 2 * i)
            return carry

        lax.fori_loop(0, looped // 2, pair, 0)
        for p in range(looped, count):
            fill(p + 2, 0, p - 1)
    else:
        for p, a in enumerate((0, 1, lats - 1)):
            fill(a, p % 2, p - 1 if p else None)
    drain(count - 1, (count - 1) % 2)


def conv_local(layer, info, band, own, near, mixes, halos=None):
    lats, reach, channels = own.shape
    inner = halos is None
    count = lats - 3 if inner else 3
    blocks = (own, near) if inner else (own, halos[0], near, halos[1])
    return pl.pallas_call(
        functools.partial(local_kernel, layer, inner),
        out_shape=jax.ShapeDtypeStruct((count, reach, channels), F32),
        in_specs=[smem()] + [vmem()] * (len(blocks) + 2),
        out_specs=vmem(),
        scratch_shapes=[pltpu.VMEM((2, band.shape[2], channels), F32)],
        compiler_params=pltpu.CompilerParams(vmem_limit_bytes=10 << 20),
        cost_estimate=pl.CostEstimate(
            flops=count << 29, bytes_accessed=count << 20, transcendentals=0
        ),
        name="conv_inner" if inner else "conv_outer",
    )(info, band, *blocks, mixes)


def post_kernel(
    layer, band, far_edge, far_body, far_halo, part_inner, part_outer, mixes, field, first, second, out, *edges_and_scratch
):
    edges, (far_ext, conv, act, hidden) = edges_and_scratch[:-4], edges_and_scratch[-4:]
    lats, reach, channels = field.shape
    far_ext[0:2] = far_halo[0:2]
    far_ext[2:3] = far_edge[2:3]
    far_ext[3:lats] = far_body[...]
    far_ext[lats : lats + 2] = far_edge[0:2]
    far_ext[lats + 2 : lats + 3] = far_halo[2:3]
    inner = lats - 3
    outer = (0, 1, lats - 1)

    def lat_of(p):
        return p + 2 if not isinstance(p, int) or p < inner else outer[p - inner]

    def drain(p, slot, o=0, w=channels):
        part = part_inner if not isinstance(p, int) or p < inner else part_outer.at[pl.ds(p - inner, 1)]
        at = p if part is part_inner else 0
        total = part[at, :, o : o + w] + mixed(conv.at[slot], mixes, layer, reach, o, w)
        row = lat_of(p) * reach
        row = row if isinstance(row, int) else pl.multiple_of(row, reach)
        act[pl.ds(row, reach), o : o + w] = gelu(total).astype(BF16)

    def fill(p, slot, last):
        a = lat_of(p)
        window = far_ext[pl.ds(a, ROWS)].reshape(ROWS * reach, channels)
        for o, w in mix_chunks(channels):
            convolve([band[a, 2]], [window], conv.at[slot], o, w)
            drain(last, 1 - slot, o, w)

    def pair(i, carry):
        fill(2 * i, 0, jnp.maximum(2 * i - 1, 0))
        fill(2 * i + 1, 1, 2 * i)
        return carry

    looped = inner // 2 * 2
    lax.fori_loop(0, looped // 2, pair, 0)
    for p in range(looped, lats):
        fill(p, p % 2, p - 1)
    drain(lats - 1, (lats - 1) % 2)
    for o, w in mix_chunks(first.shape[2]):
        up = jnp.dot(act[...], first[layer, :, o : o + w], preferred_element_type=F32)
        hidden[:, o : o + w] = gelu(up).astype(BF16)
    for o, w in mix_chunks(channels):
        update = jnp.dot(hidden[...], second[layer, :, o : o + w], preferred_element_type=F32)
        out[:, :, o : o + w] = (
            field[:, :, o : o + w].astype(F32) + update.reshape(lats, reach, w)
        ).astype(BF16)
    if edges:
        for source, target in split_rows(out, *edges):
            target[...] = source[...]


def finish(layer, last, band, far_edge, far_body, far_halo, parts, mixes, field, first, second):
    lats, reach, channels = field.shape
    counts = [lats] if last else [lats, 2, 1, 3, lats - 3]
    return pl.pallas_call(
        functools.partial(post_kernel, layer),
        out_shape=[jax.ShapeDtypeStruct((n, reach, channels), BF16) for n in counts],
        in_specs=[vmem()] * 10,
        out_specs=[vmem()] * len(counts),
        scratch_shapes=[
            pltpu.VMEM((lats + 3, reach, channels), BF16),
            pltpu.VMEM((2, band.shape[2], channels), F32),
            pltpu.VMEM((lats * reach, channels), BF16),
            pltpu.VMEM((lats * reach, first.shape[2]), BF16),
        ],
        compiler_params=pltpu.CompilerParams(vmem_limit_bytes=14 << 20),
        cost_estimate=pl.CostEstimate(
            flops=5 << 30, bytes_accessed=8 << 20, transcendentals=1 << 20
        ),
        name="finish",
    )(band, far_edge, far_body, far_halo, *parts, mixes, field, first, second)


def shards(grid_state, filter_taps, support_start, support_count, filter_mix, w_in, w_out):
    reach = grid_state.shape[1]
    layers = w_in.shape[0]
    polar, ring = lax.axis_size("polar"), lax.axis_size("azimuth")
    near_route = [(i, i ^ 1) for i in range(ring)]
    far_route = [(i, (i + 1 if i % 2 else i - 1) % ring) for i in range(ring)]
    down_route = [(i, (i + 1) % polar) for i in range(polar)]
    up_route = [(i, (i - 1) % polar) for i in range(polar)]
    here = lax.axis_index("polar")
    parity = lax.rem(lax.axis_index("azimuth"), 2).reshape(1)
    info = jnp.concatenate([support_start, support_count, parity])

    def halo_of(above, below):
        above = jnp.where(here > 0, above, jnp.zeros_like(above))
        below = jnp.where(here < polar - 1, below, jnp.zeros_like(below))
        return jnp.concatenate([above, below], axis=0)

    mixes = jnp.transpose(filter_mix, (1, 0, 2))
    field = grid_state
    down, up, edge, body, taps = fetch(field, filter_taps)
    for layer in range(layers):
        far_edge = lax.ppermute(edge, "azimuth", far_route)
        far_body = lax.ppermute(body, "azimuth", far_route)
        near = lax.ppermute(field, "azimuth", near_route)
        above = lax.ppermute(down, "polar", down_route)
        below = lax.ppermute(up, "polar", up_route)
        if layer == 0:
            band = make_bands(info, taps, reach)
        inner = conv_local(layer, info, band, field, near, mixes)
        far_above = lax.ppermute(far_edge[:2], "polar", down_route)
        far_below = lax.ppermute(far_edge[2:], "polar", up_route)
        halo = halo_of(above, below)
        near_halo = lax.ppermute(halo, "azimuth", near_route)
        outer = conv_local(layer, info, band, field, near, mixes, (halo, near_halo))
        out = finish(
            layer, layer == layers - 1, band, far_edge, far_body,
            halo_of(far_above, far_below), (inner, outer), mixes, field, w_in, w_out,
        )
        field, (down, up, edge, body) = out[0], out[1:] or (None,) * 4
    return field


def solution(mesh):
    return jax.shard_map(
        shards,
        mesh=mesh,
        in_specs=(
            P("polar", "azimuth", None),
            P("polar", None, None, None),
            P("polar"),
            P("polar"),
            P(),
            P(),
            P(),
        ),
        out_specs=P("polar", "azimuth", None),
        check_vma=False,
    )
```

time: 78.8 us -> 77.1 us (0.978); the launches traced: 78.5 us -> 76 us
  waiting for transfers between devices: 26.8 us -> 13.4 us
  starting transfers between devices: 18.4 us -> 24.5 us
  local copies, waits for them, and re-layouts: 4.2 us -> 6.85 us
  Pallas kernels: 28.5 us -> 29.6 us
  other arithmetic: 0.42 us -> 1.25 us
    ppermute x8 -> x12, waiting for transfers between devices: 26.8 us -> 13.4 us  [the longest x2 12.4 us: shards(): far_above = lax.ppermute(far_edge[:2], 'polar', down_route)]
    unnamed x21 -> x18, local copies, waits for them, and re-layouts: 2.28 us -> 6.8 us
    ppermute x2, starting transfers between devices: 3.74 us -> 7.96 us  [shards(): near_halo = lax.ppermute(halo, 'azimuth', near_route)]
    pallas_call x4 -> x7, Pallas kernels: 22.4 us -> 25.7 us  [the longest x4 13 us: conv_local(): pl.pallas_call(functools.partial(local_kernel, layer, inner), out_shape=j...]
    ppermute x2, starting transfers between devices: 0.58 us -> 3.25 us  [shards(): near = lax.ppermute(field, 'azimuth', near_route)]
    pallas_call x1, Pallas kernels: 6.09 us -> 3.9 us  [make_bands(): pl.pallas_call(functools.partial(band_kernel, reach), out_shape=jax.Shape...]
    slice x4, local copies, waits for them, and re-layouts: 1.88 us -> 0.05 us  [the longest x2 0.03 us: shards(): far_above = lax.ppermute(far_edge[:2], 'polar', down_route)]
    concatenate x0 -> x5, other arithmetic: none -> 0.87 us  [the longest x1 0.75 us: shards(): info = jnp.concatenate([support_start, support_count, parity])]
  transfers between devices with their start and end apart: 12 -> 16, of which waited for: 5 -> 4; matrix products, arithmetic and copies ran while one was open for 3% -> 2% of each run, Pallas kernels for 23% -> 25%
where the time goes in v2:
time: 77.1 us; the launch traced here: 76 us
  Pallas kernels  29.6 us (38%)
  starting transfers between devices  24.5 us (32%)
  waiting for transfers between devices  13.4 us (17%)
  local copies, waits for them, and re-layouts  6.85 us (9%)
  other arithmetic  1.25 us (2%)
    pallas_call x4, Pallas kernels, conv_local(): pl.pallas_call(functools.partial(local_kernel, layer, inner), out_shape=j...  13 us
    ppermute x2, waiting for transfers between devices, shards(): far_above = lax.ppermute(far_edge[:2], 'polar', down_route)  12.4 us
    pallas_call x2, Pallas kernels, finish(): pl.pallas_call(functools.partial(post_kernel, layer), out_shape=[jax.Shap...  10.5 us
    ppermute x2, starting transfers between devices, shards(): near_halo = lax.ppermute(halo, 'azimuth', near_route)  7.96 us
    unnamed x18, local copies, waits for them, and re-layouts  6.8 us
    pallas_call x1, Pallas kernels, make_bands(): pl.pallas_call(functools.partial(band_kernel, reach), out_shape=jax.Shape...  3.9 us
    ppermute x2, starting transfers between devices, shards(): below = lax.ppermute(up, 'polar', up_route)  3.75 us
    ppermute x2, starting transfers between devices, shards(): far_below = lax.ppermute(far_edge[2:], 'polar', up_route)  3.73 us
  transfers between devices with their start and end apart: 16, of which 4 were waited for; matrix products, arithmetic and copies ran while one was open for 2% of the time, Pallas kernels for 25%

profile of v2, /device:TPU:1, one launch (start us, length us, event | category | flops | bytes accessed | tf_op | source)
XLA Modules:
  0.0 76.0 jit_solution(3162355700675223346)
XLA Ops:
  0.0 0.0 collective-permute-start.4
  0.0 2.3 %fetch.1 = (bf16[2,64,640]{2,1,0:T(8,128)(2,1)}, bf16[1,64,640]{2,1,0:T(8,128)(2,1)}, bf16[3,64,640]{2,1,0:T(8,128)(2,1)}, bf16[5,64,640]{2,1,0:T(8,128)(2,1)}, bf16[8,9,4,129]{3,2,1,0:T(4,128)(2,1)}) custom-call(bf16[8,64,640]{2,1,0:T(8,128)(2,1)} %field.3, bf16[8,9,4,129]{3,2,1,0:T(4,128)(2,1)} %taps.1), custom_call_target="tpu_custom_call" | custom-call | bytes 1048576 | tf_op jit(solution)/shard_map/fetch/pallas_call | solution.py:130
  2.3 3.7 %collective-permute-start.6 = (bf16[1,64,640]{2,1,0:T(8,128)(2,1)}, bf16[1,64,640]{2,1,0:T(8,128)(2,1)S(1)}, u32[]{:S(2)}, u32[]{:S(2)}) collective-permute-start(bf16[1,64,640]{2,1,0:T(8,128)(2,1)} %get-tuple-element.19), channel_id=1, source_target_pairs={{0,24},{8,0},{16,8},{24,16},{1,25},{9,1},{17,9},{25,17},{2,26},{10... | collective-permute-start | bytes 245768 | tf_op jit(solution)/shard_map/ppermute | solution.py:342
  6.0 0.0 collective-permute-start.5
  6.0 1.5 %collective-permute-start = (bf16[3,64,640]{2,1,0:T(8,128)(2,1)}, bf16[3,64,640]{2,1,0:T(8,128)(2,1)S(1)}, u32[]{:S(2)}, u32[]{:S(2)}) collective-permute-start(bf16[3,64,640]{2,1,0:T(8,128)(2,1)} %get-tuple-element.16), channel_id=1, source_target_pairs={{0,7},{1,2},{2,1},{3,4},{4,3},{5,6},{6,5},{7,0},{8,15},{9,10},{10,... | collective-permute-start | bytes 737288 | tf_op jit(solution)/shard_map/ppermute | solution.py:338
  7.5 0.3 collective-permute-start.1
  7.8 0.2 fusion.table
  8.0 0.8 pad_add_fusion.info
  8.7 0.0 copy-start.6
  8.7 0.9 %copy-done.6 = bf16[8,9,4,129]{3,2,1,0:T(4,128)(2,1)S(1)} copy-done((bf16[8,9,4,129]{3,2,1,0:T(4,128)(2,1)S(1)}, bf16[8,9,4,129]{3,2,1,0:T(4,128)(2,1)}, u32[]{:S(2)}) %copy-start.6) | copy-done | bytes 74328
  9.6 0.0 copy-start.2
  9.7 0.0 copy-start.3
  9.7 3.9 %bands.1.band = bf16[8,3,576,256]{3,2,1,0:T(8,128)(2,1)S(1)} custom-call(s32[17]{0:T(128)S(1)} %pad_add_fusion.info, bf16[8,9,4,129]{3,2,1,0:T(4,128)(2,1)S(1)} %copy-done.6, bf16[2,256,768]{2,1,0:T(8,128)(2,1)S(1)} %fusion.table), custom_call_target="tpu_custom_call" | custom-call | flops 4294967296 | bytes 25165824 | tf_op jit(solution)/shard_map/bands/pallas_call | solution.py:90
  13.6 0.0 copy-start
  13.6 2.9 %copy-done = bf16[8,3,576,256]{3,2,1,0:T(8,128)(2,1)} copy-done((bf16[8,3,576,256]{3,2,1,0:T(8,128)(2,1)}, bf16[8,3,576,256]{3,2,1,0:T(8,128)(2,1)S(1)}, u32[]{:S(2)}) %copy-start) | copy-done | bytes 7077912
  16.4 0.0 collective-permute-done.6
  16.4 0.0 collective-permute-done.5
  16.5 0.0 collective-permute-done.far_edge
  16.5 2.4 %collective-permute-start.3 = (bf16[1,64,640]{2,1,0:T(8,128)(2,1)S(1)}, bf16[1,64,640]{2,1,0:T(8,128)(2,1)S(1)}, u32[]{:S(2)}, u32[]{:S(2)}) collective-permute-start(bf16[1,64,640]{2,1,0:T(8,128)(2,1)S(1)} %slice.17), channel_id=1, source_target_pairs={{0,24},{8,0},{16,8},{24,16},{1,25},{9,1},{17,9},{25,17},{2,26},{10... | collective-permute-start | bytes 245768 | tf_op jit(solution)/shard_map/ppermute | solution.py:347
  19.0 2.7 %collective-permute-start.7 = (bf16[3,64,640]{2,1,0:T(8,128)(2,1)S(1)}, bf16[3,64,640]{2,1,0:T(8,128)(2,1)S(1)}, u32[]{:S(2)}, u32[]{:S(2)}) collective-permute-start(bf16[3,64,640]{2,1,0:T(8,128)(2,1)S(1)} %pad_maximum_fusion.1.refs_1_), channel_id=1, source_target_pairs={{0,1},{1,0},{2,3},{3,2},{4,5},{5,4},{6,7},{7,6},{8,9},{9,8},{10,11... | collective-permute-start | bytes 737288 | tf_op jit(solution)/shard_map/ppermute | solution.py:349
  21.7 0.1 collective-permute-start.2
  21.7 0.0 collective-permute-done.3
  21.8 6.6 %collective-permute-done.2 = bf16[2,64,640]{2,1,0:T(8,128)(2,1)S(1)} collective-permute-done((bf16[2,64,640]{2,1,0:T(8,128)(2,1)S(1)}, bf16[2,64,640]{2,1,0:T(8,128)(2,1)S(1)}, u32[]{:S(2)}, u32[]{:S(2)}) %collective-permute-start.2) | collective-permute-done | bytes 163872 | tf_op jit(solution)/shard_map/ppermute | solution.py:346
  28.4 0.0 collective-permute-done.7.refs_3_
  28.4 0.0 collective-permute-done.4.refs_1_.refs_2_
  28.5 0.0 copy-done.2
  28.5 0.0 copy-done.3
  28.5 0.0 copy-start.1
  28.5 3.0 %copy-done.1 = bf16[8,3,576,256]{3,2,1,0:T(8,128)(2,1)S(1)} copy-done((bf16[8,3,576,256]{3,2,1,0:T(8,128)(2,1)S(1)}, bf16[8,3,576,256]{3,2,1,0:T(8,128)(2,1)}, u32[]{:S(2)}) %copy-start.1) | copy-done | bytes 7077912
  31.5 0.0 slice-start
  31.5 2.7 %conv_outer.2.part_outer = f32[3,64,640]{2,1,0:T(8,128)S(1)} custom-call(s32[17]{0:T(128)S(1)} %pad_add_fusion.info, bf16[8,3,576,256]{3,2,1,0:T(8,128)(2,1)S(1)} %copy-done.1, bf16[8,64,640]{2,1,0:T(8,128)(2,1)S(1)} %copy-done.2, bf16[3,64,640]{2,1,0:T(8,128)(2,1)S(1)} %pad_maximum_fusion.1.refs_1_, ...), custom_call_target="tpu_custom_call" | custom-call | flops 1610612736 | bytes 3145728 | tf_op jit(solution)/shard_map/conv_outer/pallas_call | solution.py:227
  34.2 0.0 slice-start.1
  34.2 0.0 copy-start.4
  34.2 0.0 copy-start.5
  34.2 3.8 %conv_inner.2.part_inner = f32[5,64,640]{2,1,0:T(8,128)S(1)} custom-call(s32[17]{0:T(128)S(1)} %pad_add_fusion.info, bf16[8,3,576,256]{3,2,1,0:T(8,128)(2,1)S(1)} %copy-done.1, bf16[8,64,640]{2,1,0:T(8,128)(2,1)S(1)} %copy-done.2, bf16[8,64,640]{2,1,0:T(8,128)(2,1)S(1)} %collective-permute-done.4.refs_1_.refs_2_, bf16[9,2,640]{2,1,0:T(2,128)(2,1)S(1)} %bitcast.5), custom_call_target="tpu_custom_call" | custom-call | flops 2684354560 | bytes 5242880 | tf_op jit(solution)/shard_map/conv_inner/pallas_call | solution.py:227
  38.0 0.0 collective-permute-done.1.far_body
  38.0 0.0 slice-done
  38.0 0.0 slice-done.1
  38.0 0.0 copy-done.4
  38.0 0.0 copy-done.5
  38.1 4.8 %finish.2 = (bf16[8,64,640]{2,1,0:T(8,128)(2,1)S(1)}, bf16[2,64,640]{2,1,0:T(8,128)(2,1)S(1)}, bf16[1,64,640]{2,1,0:T(8,128)(2,1)S(1)}, bf16[3,64,640]{2,1,0:T(8,128)(2,1)S(1)}, bf16[5,64,640]{2,1,0:T(8,128)(2,1)S(1)}) custom-call(bf16[8,3,576,256]{3,2,1,0:T(8,128)(2,1)S(1)} %bitcast.3, bf16[3,64,640]{2,1,0:T(8,128)(2,1)S(1)} %collective-permute-done.far_edge, ...), custom_call_target="tpu_custom_call" | custom-call | flops 5368709120 | bytes 8388608 | tf_op jit(solution)/shard_map/finish/pallas_call | solution.py:298
  42.9 0.1 collective-permute-start.14
  43.0 1.5 %collective-permute-start.13 = (bf16[2,64,640]{2,1,0:T(8,128)(2,1)S(1)}, bf16[2,64,640]{2,1,0:T(8,128)(2,1)S(1)}, u32[]{:S(2)}, u32[]{:S(2)}) collective-permute-start(bf16[2,64,640]{2,1,0:T(8,128)(2,1)S(1)} %get-tuple-element.23), channel_id=1, source_target_pairs={{0,8},{8,16},{16,24},{24,0},{1,9},{9,17},{17,25},{25,1},{2,10},{10... | collective-permute-start | bytes 491528 | tf_op jit(solution)/shard_map/ppermute | solution.py:341
  44.4 0.8 %collective-permute-start.8 = (bf16[3,64,640]{2,1,0:T(8,128)(2,1)S(1)}, bf16[3,64,640]{2,1,0:T(8,128)(2,1)S(1)}, u32[]{:S(2)}, u32[]{:S(2)}) collective-permute-start(bf16[3,64,640]{2,1,0:T(8,128)(2,1)S(1)} %get-tuple-element.20), channel_id=1, source_target_pairs={{0,7},{1,2},{2,1},{3,4},{4,3},{5,6},{6,5},{7,0},{8,15},{9,10},{10,... | collective-permute-start | bytes 737288 | tf_op jit(solution)/shard_map/ppermute | solution.py:338
  45.2 0.9 %collective-permute-start.9 = (bf16[5,64,640]{2,1,0:T(8,128)(2,1)S(1)}, bf16[5,64,640]{2,1,0:T(8,128)(2,1)S(1)}, u32[]{:S(2)}, u32[]{:S(2)}) collective-permute-start(bf16[5,64,640]{2,1,0:T(8,128)(2,1)S(1)} %get-tuple-element.21), channel_id=1, source_target_pairs={{0,7},{1,2},{2,1},{3,4},{4,3},{5,6},{6,5},{7,0},{8,15},{9,10},{10,... | collective-permute-start | bytes 1228808 | tf_op jit(solution)/shard_map/ppermute | solution.py:339
  46.2 3.2 %collective-permute-start.12 = (bf16[8,64,640]{2,1,0:T(8,128)(2,1)S(1)}, bf16[8,64,640]{2,1,0:T(8,128)(2,1)S(1)}, u32[]{:S(2)}, u32[]{:S(2)}) collective-permute-start(bf16[8,64,640]{2,1,0:T(8,128)(2,1)S(1)} %get-tuple-element.22.refs_0_.field), channel_id=1, source_target_pairs={{0,1},{1,0},{2,3},{3,2},{4,5},{5,4},{6,7},{7,6},{8,9},{9,8},{10,11... | collective-permute-start | bytes 1966088 | tf_op jit(solution)/shard_map/ppermute | solution.py:340
  49.4 0.0 collective-permute-done.14
  49.4 0.7 collective-permute-done.13
  50.2 0.3 collective-permute-done.8.far_edge
  50.4 1.3 %collective-permute-start.11 = (bf16[1,64,640]{2,1,0:T(8,128)(2,1)S(1)}, bf16[1,64,640]{2,1,0:T(8,128)(2,1)S(1)}, u32[]{:S(2)}, u32[]{:S(2)}) collective-permute-start(bf16[1,64,640]{2,1,0:T(8,128)(2,1)S(1)} %slice.19), channel_id=1, source_target_pairs={{0,24},{8,0},{16,8},{24,16},{1,25},{9,1},{17,9},{25,17},{2,26},{10... | collective-permute-start | bytes 245768 | tf_op jit(solution)/shard_map/ppermute | solution.py:347
  51.8 5.3 %collective-permute-start.15 = (bf16[3,64,640]{2,1,0:T(8,128)(2,1)S(1)}, bf16[3,64,640]{2,1,0:T(8,128)(2,1)S(1)}, u32[]{:S(2)}, u32[]{:S(2)}) collective-permute-start(bf16[3,64,640]{2,1,0:T(8,128)(2,1)S(1)} %pad_maximum_fusion.3.refs_1_), channel_id=1, source_target_pairs={{0,1},{1,0},{2,3},{3,2},{4,5},{5,4},{6,7},{7,6},{8,9},{9,8},{10,11... | collective-permute-start | bytes 737288 | tf_op jit(solution)/shard_map/ppermute | solution.py:349
  57.1 0.8 %collective-permute-start.10 = (bf16[2,64,640]{2,1,0:T(8,128)(2,1)S(1)}, bf16[2,64,640]{2,1,0:T(8,128)(2,1)S(1)}, u32[]{:S(2)}, u32[]{:S(2)}) collective-permute-start(bf16[2,64,640]{2,1,0:T(8,128)(2,1)S(1)} %slice.18), channel_id=1, source_target_pairs={{0,8},{8,16},{16,24},{24,0},{1,9},{9,17},{17,25},{25,1},{2,10},{10... | collective-permute-start | bytes 491528 | tf_op jit(solution)/shard_map/ppermute | solution.py:346
  57.9 0.0 collective-permute-done.11
  57.9 5.8 %collective-permute-done.10 = bf16[2,64,640]{2,1,0:T(8,128)(2,1)S(1)} collective-permute-done((bf16[2,64,640]{2,1,0:T(8,128)(2,1)S(1)}, bf16[2,64,640]{2,1,0:T(8,128)(2,1)S(1)}, u32[]{:S(2)}, u32[]{:S(2)}) %collective-permute-start.10) | collective-permute-done | bytes 163872 | tf_op jit(solution)/shard_map/ppermute | solution.py:346
  63.8 0.0 collective-permute-done.15.refs_3_
  63.8 0.0 collective-permute-done.12.refs_1_.refs_2_
  63.8 2.7 %conv_outer.3.part_outer = f32[3,64,640]{2,1,0:T(8,128)S(1)} custom-call(s32[17]{0:T(128)S(1)} %pad_add_fusion.info, bf16[8,3,576,256]{3,2,1,0:T(8,128)(2,1)S(1)} %bitcast.3, bf16[8,64,640]{2,1,0:T(8,128)(2,1)S(1)} %get-tuple-element.22.refs_0_.field, bf16[3,64,640]{2,1,0:T(8,128)(2,1)S(1)} %pad_maximum_fusion.3.refs_1_, ...), custom_call_target="tpu_custom_call" | custom-call | flops 1610612736 | bytes 3145728 | tf_op jit(solution)/shard_map/conv_outer/pallas_call | solution.py:227
  66.5 3.8 %conv_inner.3.part_inner = f32[5,64,640]{2,1,0:T(8,128)S(1)} custom-call(s32[17]{0:T(128)S(1)} %pad_add_fusion.info, bf16[8,3,576,256]{3,2,1,0:T(8,128)(2,1)S(1)} %bitcast.3, bf16[8,64,640]{2,1,0:T(8,128)(2,1)S(1)} %get-tuple-element.22.refs_0_.field, bf16[8,64,640]{2,1,0:T(8,128)(2,1)S(1)} %collective-permute-done.12.refs_1_.refs_2_, ...), custom_call_target="tpu_custom_call" | custom-call | flops 2684354560 | bytes 5242880 | tf_op jit(solution)/shard_map/conv_inner/pallas_call | solution.py:227
  70.4 0.0 collective-permute-done.9.far_body
  70.4 5.6 %finish.3 = bf16[8,64,640]{2,1,0:T(8,128)(2,1)} custom-call(bf16[8,3,576,256]{3,2,1,0:T(8,128)(2,1)S(1)} %bitcast.3, bf16[3,64,640]{2,1,0:T(8,128)(2,1)S(1)} %collective-permute-done.8.far_edge, bf16[5,64,640]{2,1,0:T(8,128)(2,1)S(1)} %collective-permute-done.9.far_body, bf16[3,64,640]{2,1,0:T(8,128)(2,1)S(1)} %pad_maximum_fusion.2.far_halo, ...), custom_call_target="tpu_custom_call" | custom-call | flops 5368709120 | bytes 8388608 | tf_op jit(solution)/shard_map/finish/pallas_call | solution.py:298
  (20 shorter events, 0.3 us)
Async XLA Ops:
  0.0 28.4 %collective-permute-start.4 = (bf16[8,64,640]{2,1,0:T(8,128)(2,1)}, bf16[8,64,640]{2,1,0:T(8,128)(2,1)S(1)}, u32[]{:S(2)}, u32[]{:S(2)}) collective-permute-start(bf16[8,64,640]{2,1,0:T(8,128)(2,1)} %field.3), channel_id=1, source_target_pairs={{0,1},{1,0},{2,3},{3,2},{4,5},{5,4},{6,7},{7,6},{8,9},{9,8},{10,11... | collective-permute-start | bytes 1966088 | tf_op jit(solution)/shard_map/ppermute | solution.py:340
  2.3 14.1 %collective-permute-start.6 = (bf16[1,64,640]{2,1,0:T(8,128)(2,1)}, bf16[1,64,640]{2,1,0:T(8,128)(2,1)S(1)}, u32[]{:S(2)}, u32[]{:S(2)}) collective-permute-start(bf16[1,64,640]{2,1,0:T(8,128)(2,1)} %get-tuple-element.19), channel_id=1, source_target_pairs={{0,24},{8,0},{16,8},{24,16},{1,25},{9,1},{17,9},{25,17},{2,26},{10... | collective-permute-start | bytes 245768 | tf_op jit(solution)/shard_map/ppermute | solution.py:342
  6.0 10.4 %collective-permute-start.5 = (bf16[2,64,640]{2,1,0:T(8,128)(2,1)}, bf16[2,64,640]{2,1,0:T(8,128)(2,1)S(1)}, u32[]{:S(2)}, u32[]{:S(2)}) collective-permute-start(bf16[2,64,640]{2,1,0:T(8,128)(2,1)} %get-tuple-element.18), channel_id=1, source_target_pairs={{0,8},{8,16},{16,24},{24,0},{1,9},{9,17},{17,25},{25,1},{2,10},{10... | collective-permute-start | bytes 491528 | tf_op jit(solution)/shard_map/ppermute | solution.py:341
  6.0 10.5 %collective-permute-start = (bf16[3,64,640]{2,1,0:T(8,128)(2,1)}, bf16[3,64,640]{2,1,0:T(8,128)(2,1)S(1)}, u32[]{:S(2)}, u32[]{:S(2)}) collective-permute-start(bf16[3,64,640]{2,1,0:T(8,128)(2,1)} %get-tuple-element.16), channel_id=1, source_target_pairs={{0,7},{1,2},{2,1},{3,4},{4,3},{5,6},{6,5},{7,0},{8,15},{9,10},{10,... | collective-permute-start | bytes 737288 | tf_op jit(solution)/shard_map/ppermute | solution.py:338
  7.5 30.5 %collective-permute-start.1 = (bf16[5,64,640]{2,1,0:T(8,128)(2,1)}, bf16[5,64,640]{2,1,0:T(8,128)(2,1)S(1)}, u32[]{:S(2)}, u32[]{:S(2)}) collective-permute-start(bf16[5,64,640]{2,1,0:T(8,128)(2,1)} %get-tuple-element.17), channel_id=1, source_target_pairs={{0,7},{1,2},{2,1},{3,4},{4,3},{5,6},{6,5},{7,0},{8,15},{9,10},{10,... | collective-permute-start | bytes 1228808 | tf_op jit(solution)/shard_map/ppermute | solution.py:339
  8.7 0.9 %copy-start.6 = (bf16[8,9,4,129]{3,2,1,0:T(4,128)(2,1)S(1)}, bf16[8,9,4,129]{3,2,1,0:T(4,128)(2,1)}, u32[]{:S(2)}) copy-start(bf16[8,9,4,129]{3,2,1,0:T(4,128)(2,1)} %get-tuple-element.15.taps) | copy-start | bytes 222916
  9.6 18.8 %copy-start.2 = (bf16[8,64,640]{2,1,0:T(8,128)(2,1)S(1)}, bf16[8,64,640]{2,1,0:T(8,128)(2,1)}, u32[]{:S(2)}) copy-start(bf16[8,64,640]{2,1,0:T(8,128)(2,1)} %field.3) | copy-start | bytes 1966084
  9.7 18.8 %copy-start.3 = (bf16[2,9,640]{2,0,1:T(2,128)(2,1)S(1)}, bf16[2,9,640]{2,0,1:T(2,128)(2,1)}, u32[]{:S(2)}) copy-start(bf16[2,9,640]{2,0,1:T(2,128)(2,1)} %param.11) | copy-start | bytes 69124
  13.6 2.9 %copy-start = (bf16[8,3,576,256]{3,2,1,0:T(8,128)(2,1)}, bf16[8,3,576,256]{3,2,1,0:T(8,128)(2,1)S(1)}, u32[]{:S(2)}) copy-start(bf16[8,3,576,256]{3,2,1,0:T(8,128)(2,1)S(1)} %bands.1.band) | copy-start | bytes 21233668
  16.5 5.2 %collective-permute-start.3 = (bf16[1,64,640]{2,1,0:T(8,128)(2,1)S(1)}, bf16[1,64,640]{2,1,0:T(8,128)(2,1)S(1)}, u32[]{:S(2)}, u32[]{:S(2)}) collective-permute-start(bf16[1,64,640]{2,1,0:T(8,128)(2,1)S(1)} %slice.17), channel_id=1, source_target_pairs={{0,24},{8,0},{16,8},{24,16},{1,25},{9,1},{17,9},{25,17},{2,26},{10... | collective-permute-start | bytes 245768 | tf_op jit(solution)/shard_map/ppermute | solution.py:347
  19.0 9.5 %collective-permute-start.7 = (bf16[3,64,640]{2,1,0:T(8,128)(2,1)S(1)}, bf16[3,64,640]{2,1,0:T(8,128)(2,1)S(1)}, u32[]{:S(2)}, u32[]{:S(2)}) collective-permute-start(bf16[3,64,640]{2,1,0:T(8,128)(2,1)S(1)} %pad_maximum_fusion.1.refs_1_), channel_id=1, source_target_pairs={{0,1},{1,0},{2,3},{3,2},{4,5},{5,4},{6,7},{7,6},{8,9},{9,8},{10,11... | collective-permute-start | bytes 737288 | tf_op jit(solution)/shard_map/ppermute | solution.py:349
  21.7 6.7 %collective-permute-start.2 = (bf16[2,64,640]{2,1,0:T(8,128)(2,1)S(1)}, bf16[2,64,640]{2,1,0:T(8,128)(2,1)S(1)}, u32[]{:S(2)}, u32[]{:S(2)}) collective-permute-start(bf16[2,64,640]{2,1,0:T(8,128)(2,1)S(1)} %slice.16), channel_id=1, source_target_pairs={{0,8},{8,16},{16,24},{24,0},{1,9},{9,17},{17,25},{25,1},{2,10},{10... | collective-permute-start | bytes 491528 | tf_op jit(solution)/shard_map/ppermute | solution.py:346
  28.5 3.0 %copy-start.1 = (bf16[8,3,576,256]{3,2,1,0:T(8,128)(2,1)S(1)}, bf16[8,3,576,256]{3,2,1,0:T(8,128)(2,1)}, u32[]{:S(2)}) copy-start(bf16[8,3,576,256]{3,2,1,0:T(8,128)(2,1)} %copy-done) | copy-start | bytes 21233668
  31.5 6.5 %slice-start = ((s8[7077888]{0:T(1024)(128)(4,1)}), s8[4194304]{0:T(1024)(128)(4,1)S(1)}, s32[]{:S(2)}) async-start(s8[7077888]{0:T(1024)(128)(4,1)} %bitcast.2), calls=%async_computation | async-start | bytes 8388608
  34.2 3.9 %slice-start.1 = ((s8[7077888]{0:T(1024)(128)(4,1)}), s8[2883584]{0:T(1024)(128)(4,1)S(1)}, s32[]{:S(2)}) async-start(s8[7077888]{0:T(1024)(128)(4,1)} %bitcast.2), calls=%async_computation.1 | async-start | bytes 5767168
  34.2 3.9 %copy-start.4 = (bf16[2,640,1280]{2,1,0:T(8,128)(2,1)S(1)}, bf16[2,640,1280]{2,1,0:T(8,128)(2,1)}, u32[]{:S(2)}) copy-start(bf16[2,640,1280]{2,1,0:T(8,128)(2,1)} %first.3) | copy-start | bytes 9830404
  34.2 3.9 %copy-start.5 = (bf16[2,1280,640]{2,1,0:T(8,128)(2,1)S(1)}, bf16[2,1280,640]{2,1,0:T(8,128)(2,1)}, u32[]{:S(2)}) copy-start(bf16[2,1280,640]{2,1,0:T(8,128)(2,1)} %second.3) | copy-start | bytes 9830404
  42.9 6.5 %collective-permute-start.14 = (bf16[1,64,640]{2,1,0:T(8,128)(2,1)S(1)}, bf16[1,64,640]{2,1,0:T(8,128)(2,1)S(1)}, u32[]{:S(2)}, u32[]{:S(2)}) collective-permute-start(bf16[1,64,640]{2,1,0:T(8,128)(2,1)S(1)} %get-tuple-element.24), channel_id=1, source_target_pairs={{0,24},{8,0},{16,8},{24,16},{1,25},{9,1},{17,9},{25,17},{2,26},{10... | collective-permute-start | bytes 245768 | tf_op jit(solution)/shard_map/ppermute | solution.py:342
  43.0 7.2 %collective-permute-start.13 = (bf16[2,64,640]{2,1,0:T(8,128)(2,1)S(1)}, bf16[2,64,640]{2,1,0:T(8,128)(2,1)S(1)}, u32[]{:S(2)}, u32[]{:S(2)}) collective-permute-start(bf16[2,64,640]{2,1,0:T(8,128)(2,1)S(1)} %get-tuple-element.23), channel_id=1, source_target_pairs={{0,8},{8,16},{16,24},{24,0},{1,9},{9,17},{17,25},{25,1},{2,10},{10... | collective-permute-start | bytes 491528 | tf_op jit(solution)/shard_map/ppermute | solution.py:341
  44.4 6.0 %collective-permute-start.8 = (bf16[3,64,640]{2,1,0:T(8,128)(2,1)S(1)}, bf16[3,64,640]{2,1,0:T(8,128)(2,1)S(1)}, u32[]{:S(2)}, u32[]{:S(2)}) collective-permute-start(bf16[3,64,640]{2,1,0:T(8,128)(2,1)S(1)} %get-tuple-element.20), channel_id=1, source_target_pairs={{0,7},{1,2},{2,1},{3,4},{4,3},{5,6},{6,5},{7,0},{8,15},{9,10},{10,... | collective-permute-start | bytes 737288 | tf_op jit(solution)/shard_map/ppermute | solution.py:338
  45.2 25.1 %collective-permute-start.9 = (bf16[5,64,640]{2,1,0:T(8,128)(2,1)S(1)}, bf16[5,64,640]{2,1,0:T(8,128)(2,1)S(1)}, u32[]{:S(2)}, u32[]{:S(2)}) collective-permute-start(bf16[5,64,640]{2,1,0:T(8,128)(2,1)S(1)} %get-tuple-element.21), channel_id=1, source_target_pairs={{0,7},{1,2},{2,1},{3,4},{4,3},{5,6},{6,5},{7,0},{8,15},{9,10},{10,... | collective-permute-start | bytes 1228808 | tf_op jit(solution)/shard_map/ppermute | solution.py:339
  46.2 17.7 %collective-permute-start.12 = (bf16[8,64,640]{2,1,0:T(8,128)(2,1)S(1)}, bf16[8,64,640]{2,1,0:T(8,128)(2,1)S(1)}, u32[]{:S(2)}, u32[]{:S(2)}) collective-permute-start(bf16[8,64,640]{2,1,0:T(8,128)(2,1)S(1)} %get-tuple-element.22.refs_0_.field), channel_id=1, source_target_pairs={{0,1},{1,0},{2,3},{3,2},{4,5},{5,4},{6,7},{7,6},{8,9},{9,8},{10,11... | collective-permute-start | bytes 1966088 | tf_op jit(solution)/shard_map/ppermute | solution.py:340
  50.4 7.5 %collective-permute-start.11 = (bf16[1,64,640]{2,1,0:T(8,128)(2,1)S(1)}, bf16[1,64,640]{2,1,0:T(8,128)(2,1)S(1)}, u32[]{:S(2)}, u32[]{:S(2)}) collective-permute-start(bf16[1,64,640]{2,1,0:T(8,128)(2,1)S(1)} %slice.19), channel_id=1, source_target_pairs={{0,24},{8,0},{16,8},{24,16},{1,25},{9,1},{17,9},{25,17},{2,26},{10... | collective-permute-start | bytes 245768 | tf_op jit(solution)/shard_map/ppermute | solution.py:347
  51.8 12.0 %collective-permute-start.15 = (bf16[3,64,640]{2,1,0:T(8,128)(2,1)S(1)}, bf16[3,64,640]{2,1,0:T(8,128)(2,1)S(1)}, u32[]{:S(2)}, u32[]{:S(2)}) collective-permute-start(bf16[3,64,640]{2,1,0:T(8,128)(2,1)S(1)} %pad_maximum_fusion.3.refs_1_), channel_id=1, source_target_pairs={{0,1},{1,0},{2,3},{3,2},{4,5},{5,4},{6,7},{7,6},{8,9},{9,8},{10,11... | collective-permute-start | bytes 737288 | tf_op jit(solution)/shard_map/ppermute | solution.py:349
  57.1 6.7 %collective-permute-start.10 = (bf16[2,64,640]{2,1,0:T(8,128)(2,1)S(1)}, bf16[2,64,640]{2,1,0:T(8,128)(2,1)S(1)}, u32[]{:S(2)}, u32[]{:S(2)}) collective-permute-start(bf16[2,64,640]{2,1,0:T(8,128)(2,1)S(1)} %slice.18), channel_id=1, source_target_pairs={{0,8},{8,16},{16,24},{24,0},{1,9},{9,17},{17,25},{25,1},{2,10},{10... | collective-permute-start | bytes 491528 | tf_op jit(solution)/shard_map/ppermute | solution.py:346

commit v3 on v2

--- a/solution.py
+++ b/solution.py
@@ -45,25 +45,27 @@
     rows[...] = jnp.zeros_like(rows)
     lane = lax.broadcasted_iota(jnp.int32, (ROWS, tap_count), 1) - reach
 
-    def skewed(a, carry):
+    def masked(a, carry):
         inside = (lane >= info[a]) & (lane < info[a] + info[lats + a])
         for k in range(filters):
-            rows[k, 0:ROWS, 0:tap_count] = jnp.where(inside, taps[a, k].astype(F32), 0.0)
-        for k in range(filters):
-            at = pl.ds(pl.multiple_of(a * block + k * STRIP, STRIP), STRIP)
-            for r in range(ROWS):
-                skew = pltpu.roll(
-                    jnp.broadcast_to(rows[k, r : r + 1, :], (STRIP, wide)),
-                    0, 1, stride=1, stride_axis=0,
-                )
-                base[r, at, :] = skew.astype(BF16)
+            rows[a, k, 0:ROWS, 0:tap_count] = jnp.where(inside, taps[a, k].astype(F32), 0.0)
         return carry
 
-    lax.fori_loop(0, lats, skewed, 0)
+    lax.fori_loop(0, lats, masked, 0)
+
+    def skew(r):
+        for a in range(lats):
+            for k in range(filters):
+                at = a * block + k * STRIP
+                row = jnp.broadcast_to(rows[a, k, r : r + 1, :], (STRIP, wide))
+                base[r, at : at + STRIP, :] = pltpu.roll(row, 0, 1, stride=1, stride_axis=0).astype(BF16)
+
     low = lax.broadcasted_iota(jnp.int32, (lats * block, 2 * reach), 1) < reach
-    for s in range(3):
-        columns = slice(s * strips * reach, (s + 1) * strips * reach)
-        for pair in range(ROWS // 2):
+    for pair in range(ROWS // 2):
+        skew(2 * pair)
+        skew(2 * pair + 1)
+        for s in range(3):
+            columns = slice(s * strips * reach, (s + 1) * strips * reach)
             even, odd = (
                 jnp.dot(base[2 * pair + m], table[m, :, columns], preferred_element_type=F32).astype(BF16)
                 for m in range(2)
@@ -93,7 +95,7 @@
         in_specs=[smem(), vmem(), vmem()],
         out_specs=vmem(),
         scratch_shapes=[
-            pltpu.VMEM((filters, 8, 4 * reach), F32),
+            pltpu.VMEM((lats, filters, 8, 4 * reach), F32),
             pltpu.VMEM((ROWS, lats * filters * STRIP, 4 * reach), BF16),
         ],
         compiler_params=pltpu.CompilerParams(vmem_limit_bytes=12 << 20),
@@ -116,8 +118,8 @@
     ]
 
 
-def fetch_kernel(field, taps, down, up, edge, body, taps_out, sem):
-    moves = split_rows(field, down, up, edge, body) + [(taps, taps_out)]
+def fetch_kernel(field, down, up, edge, body, sem):
+    moves = split_rows(field, down, up, edge, body)
     moves = [pltpu.make_async_copy(s, d, sem.at[i]) for i, (s, d) in enumerate(moves)]
     for m in moves:
         m.start()
@@ -125,18 +127,18 @@
         m.wait()
 
 
-def fetch(field, taps):
-    shapes = [(n,) + field.shape[1:] for n in (2, 1, 3, field.shape[0] - 3)] + [taps.shape]
+def fetch(field):
+    shapes = [(n,) + field.shape[1:] for n in (2, 1, 3, field.shape[0] - 3)]
     return pl.pallas_call(
         fetch_kernel,
         out_shape=[jax.ShapeDtypeStruct(s, BF16) for s in shapes],
-        in_specs=[pl.BlockSpec(memory_space=pl.ANY)] * 2,
+        in_specs=[pl.BlockSpec(memory_space=pl.ANY)],
         out_specs=[vmem()] * len(shapes),
-        scratch_shapes=[pltpu.SemaphoreType.DMA((6,))],
-        compiler_params=pltpu.CompilerParams(vmem_limit_bytes=60 << 20),
+        scratch_shapes=[pltpu.SemaphoreType.DMA((5,))],
+        compiler_params=pltpu.CompilerParams(vmem_limit_bytes=4 << 20),
         cost_estimate=pl.CostEstimate(flops=0, bytes_accessed=1 << 20, transcendentals=0),
         name="fetch",
-    )(field, taps)
+    )(field)
 
 
 def mix_chunks(channels):
@@ -239,9 +241,11 @@
 
 
 def post_kernel(
-    layer, band, far_edge, far_body, far_halo, part_inner, part_outer, mixes, field, first, second, out, *edges_and_scratch
+    layer, last, band, far_edge, far_body, far_halo, part_inner, part_outer, mixes, field, first, second, result, *edges_and_scratch
 ):
-    edges, (far_ext, conv, act, hidden) = edges_and_scratch[:-4], edges_and_scratch[-4:]
+    edges = edges_and_scratch[: 0 if last else 4]
+    far_ext, conv, act, hidden, *rest = edges_and_scratch[len(edges) :]
+    out, sent = rest if last else (result, None)
     lats, reach, channels = field.shape
     far_ext[0:2] = far_halo[0:2]
     far_ext[2:3] = far_edge[2:3]
@@ -282,11 +286,18 @@
     for o, w in mix_chunks(first.shape[2]):
         up = jnp.dot(act[...], first[layer, :, o : o + w], preferred_element_type=F32)
         hidden[:, o : o + w] = gelu(up).astype(BF16)
+    sends = []
     for o, w in mix_chunks(channels):
         update = jnp.dot(hidden[...], second[layer, :, o : o + w], preferred_element_type=F32)
         out[:, :, o : o + w] = (
             field[:, :, o : o + w].astype(F32) + update.reshape(lats, reach, w)
         ).astype(BF16)
+        if last:
+            part = (slice(None), slice(None), pl.ds(o, w))
+            sends.append(pltpu.make_async_copy(out.at[part], result.at[part], sent.at[len(sends)]))
+            sends[-1].start()
+    for send in sends:
+        send.wait()
     if edges:
         for source, target in split_rows(out, *edges):
             target[...] = source[...]
@@ -296,16 +307,21 @@
     lats, reach, channels = field.shape
     counts = [lats] if last else [lats, 2, 1, 3, lats - 3]
     return pl.pallas_call(
-        functools.partial(post_kernel, layer),
+        functools.partial(post_kernel, layer, last),
         out_shape=[jax.ShapeDtypeStruct((n, reach, channels), BF16) for n in counts],
         in_specs=[vmem()] * 10,
-        out_specs=[vmem()] * len(counts),
+        out_specs=[pl.BlockSpec(memory_space=pl.ANY)] if last else [vmem()] * len(counts),
         scratch_shapes=[
             pltpu.VMEM((lats + 3, reach, channels), BF16),
             pltpu.VMEM((2, band.shape[2], channels), F32),
             pltpu.VMEM((lats * reach, channels), BF16),
             pltpu.VMEM((lats * reach, first.shape[2]), BF16),
-        ],
+        ]
+        + (
+            [pltpu.VMEM(field.shape, BF16), pltpu.SemaphoreType.DMA((len(mix_chunks(channels)),))]
+            if last
+            else []
+        ),
         compiler_params=pltpu.CompilerParams(vmem_limit_bytes=14 << 20),
         cost_estimate=pl.CostEstimate(
             flops=5 << 30, bytes_accessed=8 << 20, transcendentals=1 << 20
@@ -333,7 +349,7 @@
 
     mixes = jnp.transpose(filter_mix, (1, 0, 2))
     field = grid_state
-    down, up, edge, body, taps = fetch(field, filter_taps)
+    down, up, edge, body = fetch(field)
     for layer in range(layers):
         far_edge = lax.ppermute(edge, "azimuth", far_route)
         far_body = lax.ppermute(body, "azimuth", far_route)
@@ -341,7 +357,7 @@
         above = lax.ppermute(down, "polar", down_route)
         below = lax.ppermute(up, "polar", up_route)
         if layer == 0:
-            band = make_bands(info, taps, reach)
+            band = make_bands(info, filter_taps, reach)
         inner = conv_local(layer, info, band, field, near, mixes)
         far_above = lax.ppermute(far_edge[:2], "polar", down_route)
         far_below = lax.ppermute(far_edge[2:], "polar", up_route)

time: 77.1 us -> 75.9 us (0.984)
  Pallas kernels: 29.6 us -> 27.2 us
  local copies, waits for them, and re-layouts: 6.85 us -> 7.93 us
    pallas_call x1, Pallas kernels: 2.28 us -> 0.86 us  [fetch(): pl.pallas_call(fetch_kernel, out_shape=[jax.ShapeDtypeStruct(s, BF16) for...]
    unnamed x18 -> x20, local copies, waits for them, and re-layouts: 6.8 us -> 7.88 us
    pallas_call x1, Pallas kernels: 3.9 us -> 3.05 us  [make_bands(): pl.pallas_call(functools.partial(band_kernel, reach), out_shape=jax.Shape...]
  transfers between devices with their start and end apart: 16 -> 16, of which waited for: 4 -> 4; matrix products, arithmetic and copies ran while one was open for 2% -> 2% of each run, Pallas kernels for 25% -> 23%
where the time goes in v3:
time: 75.9 us; the launch traced here: 74.8 us
  Pallas kernels  27.2 us (36%)
  starting transfers between devices  24.5 us (32%)
  waiting for transfers between devices  13.4 us (18%)
  local copies, waits for them, and re-layouts  7.93 us (10%)
  other arithmetic  1.25 us (2%)
    pallas_call x4, Pallas kernels, conv_local(): pl.pallas_call(functools.partial(local_kernel, layer, inner), out_shape=j...  13 us
    ppermute x2, waiting for transfers between devices, shards(): far_above = lax.ppermute(far_edge[:2], 'polar', down_route)  12.4 us
    pallas_call x2, Pallas kernels, finish(): pl.pallas_call(functools.partial(post_kernel, layer, last), out_shape=[ja...  10.3 us
    ppermute x2, starting transfers between devices, shards(): near_halo = lax.ppermute(halo, 'azimuth', near_route)  7.94 us
    unnamed x20, local copies, waits for them, and re-layouts  7.88 us
    ppermute x2, starting transfers between devices, shards(): below = lax.ppermute(up, 'polar', up_route)  3.75 us
    ppermute x2, starting transfers between devices, shards(): far_below = lax.ppermute(far_edge[2:], 'polar', up_route)  3.73 us
    ppermute x2, starting transfers between devices, shards(): near = lax.ppermute(field, 'azimuth', near_route)  3.24 us
  transfers between devices with their start and end apart: 16, of which 4 were waited for; matrix products, arithmetic and copies ran while one was open for 2% of the time, Pallas kernels for 23%

profile of v3, /device:TPU:1, one launch (start us, length us, event | category | flops | bytes accessed | tf_op | source)
XLA Modules:
  0.0 74.8 jit_solution(4796246503641814652)
XLA Ops:
  0.0 0.0 collective-permute-start.4
  0.0 0.0 copy-start.2
  0.0 1.1 %copy-done.2 = bf16[8,64,640]{2,1,0:T(8,128)(2,1)S(1)} copy-done((bf16[8,64,640]{2,1,0:T(8,128)(2,1)S(1)}, bf16[8,64,640]{2,1,0:T(8,128)(2,1)}, u32[]{:S(2)}) %copy-start.2) | copy-done | bytes 655384
  1.1 0.9 %fetch.1 = (bf16[2,64,640]{2,1,0:T(8,128)(2,1)S(1)}, bf16[1,64,640]{2,1,0:T(8,128)(2,1)S(1)}, bf16[3,64,640]{2,1,0:T(8,128)(2,1)S(1)}, bf16[5,64,640]{2,1,0:T(8,128)(2,1)S(1)}) custom-call(bf16[8,64,640]{2,1,0:T(8,128)(2,1)S(1)} %copy-done.2), custom_call_target="tpu_custom_call" | custom-call | bytes 1048576 | tf_op jit(solution)/shard_map/fetch/pallas_call | solution.py:132
  2.0 3.7 %collective-permute-start.6 = (bf16[1,64,640]{2,1,0:T(8,128)(2,1)S(1)}, bf16[1,64,640]{2,1,0:T(8,128)(2,1)S(1)}, u32[]{:S(2)}, u32[]{:S(2)}) collective-permute-start(bf16[1,64,640]{2,1,0:T(8,128)(2,1)S(1)} %get-tuple-element.17), channel_id=1, source_target_pairs={{0,24},{8,0},{16,8},{24,16},{1,25},{9,1},{17,9},{25,17},{2,26},{10... | collective-permute-start | bytes 245768 | tf_op jit(solution)/shard_map/ppermute | solution.py:358
  5.7 0.0 collective-permute-start.5
  5.7 1.5 %collective-permute-start = (bf16[3,64,640]{2,1,0:T(8,128)(2,1)S(1)}, bf16[3,64,640]{2,1,0:T(8,128)(2,1)S(1)}, u32[]{:S(2)}, u32[]{:S(2)}) collective-permute-start(bf16[3,64,640]{2,1,0:T(8,128)(2,1)S(1)} %get-tuple-element.14), channel_id=1, source_target_pairs={{0,7},{1,2},{2,1},{3,4},{4,3},{5,6},{6,5},{7,0},{8,15},{9,10},{10,... | collective-permute-start | bytes 737288 | tf_op jit(solution)/shard_map/ppermute | solution.py:354
  7.1 0.3 collective-permute-start.1
  7.5 0.2 fusion.table
  7.7 0.8 %pad_add_fusion.info = s32[17]{0:T(128)S(1)} fusion(s32[1]{0:T(128)} %bitcast, s32[8]{0:T(128)} %param.10, s32[8]{0:T(128)} %param.9), kind=kLoop, calls=%fused_computation.44 | loop fusion | flops 34 | bytes 136 | tf_op jit(solution)/shard_map/concatenate | solution.py:343
  8.4 0.0 copy-start.7
  8.4 0.9 %copy-done.7 = bf16[8,9,4,129]{3,2,1,0:T(4,128)(2,1)S(1)} copy-done((bf16[8,9,4,129]{3,2,1,0:T(4,128)(2,1)S(1)}, bf16[8,9,4,129]{3,2,1,0:T(4,128)(2,1)}, u32[]{:S(2)}) %copy-start.7) | copy-done | bytes 74328
  9.3 0.0 copy-start.3
  9.3 0.0 copy-start.4
  9.3 3.1 %bands.1.band = bf16[8,3,576,256]{3,2,1,0:T(8,128)(2,1)S(1)} custom-call(s32[17]{0:T(128)S(1)} %pad_add_fusion.info, bf16[8,9,4,129]{3,2,1,0:T(4,128)(2,1)S(1)} %copy-done.7, bf16[2,256,768]{2,1,0:T(8,128)(2,1)S(1)} %fusion.table), custom_call_target="tpu_custom_call" | custom-call | flops 4294967296 | bytes 25165824 | tf_op jit(solution)/shard_map/bands/pallas_call | solution.py:92
  12.4 0.0 copy-start
  12.4 2.9 %copy-done = bf16[8,3,576,256]{3,2,1,0:T(8,128)(2,1)} copy-done((bf16[8,3,576,256]{3,2,1,0:T(8,128)(2,1)}, bf16[8,3,576,256]{3,2,1,0:T(8,128)(2,1)S(1)}, u32[]{:S(2)}) %copy-start) | copy-done | bytes 7077912
  15.2 0.0 collective-permute-done.6
  15.3 0.0 collective-permute-done.5
  15.3 0.0 collective-permute-done.far_edge
  15.3 2.4 %collective-permute-start.3 = (bf16[1,64,640]{2,1,0:T(8,128)(2,1)S(1)}, bf16[1,64,640]{2,1,0:T(8,128)(2,1)S(1)}, u32[]{:S(2)}, u32[]{:S(2)}) collective-permute-start(bf16[1,64,640]{2,1,0:T(8,128)(2,1)S(1)} %slice.17), channel_id=1, source_target_pairs={{0,24},{8,0},{16,8},{24,16},{1,25},{9,1},{17,9},{25,17},{2,26},{10... | collective-permute-start | bytes 245768 | tf_op jit(solution)/shard_map/ppermute | solution.py:363
  17.8 2.7 %collective-permute-start.7 = (bf16[3,64,640]{2,1,0:T(8,128)(2,1)S(1)}, bf16[3,64,640]{2,1,0:T(8,128)(2,1)S(1)}, u32[]{:S(2)}, u32[]{:S(2)}) collective-permute-start(bf16[3,64,640]{2,1,0:T(8,128)(2,1)S(1)} %pad_maximum_fusion.1.refs_1_), channel_id=1, source_target_pairs={{0,1},{1,0},{2,3},{3,2},{4,5},{5,4},{6,7},{7,6},{8,9},{9,8},{10,11... | collective-permute-start | bytes 737288 | tf_op jit(solution)/shard_map/ppermute | solution.py:365
  20.5 0.1 collective-permute-start.2
  20.6 0.0 collective-permute-done.3
  20.6 6.6 %collective-permute-done.2 = bf16[2,64,640]{2,1,0:T(8,128)(2,1)S(1)} collective-permute-done((bf16[2,64,640]{2,1,0:T(8,128)(2,1)S(1)}, bf16[2,64,640]{2,1,0:T(8,128)(2,1)S(1)}, u32[]{:S(2)}, u32[]{:S(2)}) %collective-permute-start.2) | collective-permute-done | bytes 163872 | tf_op jit(solution)/shard_map/ppermute | solution.py:362
  27.3 0.0 collective-permute-done.7.refs_3_
  27.3 0.0 collective-permute-done.4.refs_1_.refs_2_
  27.3 0.0 copy-done.3
  27.3 0.0 copy-done.4
  27.3 0.0 copy-start.1
  27.3 3.0 %copy-done.1 = bf16[8,3,576,256]{3,2,1,0:T(8,128)(2,1)S(1)} copy-done((bf16[8,3,576,256]{3,2,1,0:T(8,128)(2,1)S(1)}, bf16[8,3,576,256]{3,2,1,0:T(8,128)(2,1)}, u32[]{:S(2)}) %copy-start.1) | copy-done | bytes 7077912
  30.3 0.0 slice-start
  30.3 2.7 %conv_outer.2.part_outer = f32[3,64,640]{2,1,0:T(8,128)S(1)} custom-call(s32[17]{0:T(128)S(1)} %pad_add_fusion.info, bf16[8,3,576,256]{3,2,1,0:T(8,128)(2,1)S(1)} %copy-done.1, bf16[8,64,640]{2,1,0:T(8,128)(2,1)S(1)} %copy-done.3, bf16[3,64,640]{2,1,0:T(8,128)(2,1)S(1)} %pad_maximum_fusion.1.refs_1_, ...), custom_call_target="tpu_custom_call" | custom-call | flops 1610612736 | bytes 3145728 | tf_op jit(solution)/shard_map/conv_outer/pallas_call | solution.py:229
  33.0 0.0 slice-start.1
  33.0 0.0 copy-start.5
  33.0 0.0 copy-start.6
  33.0 3.8 %conv_inner.2.part_inner = f32[5,64,640]{2,1,0:T(8,128)S(1)} custom-call(s32[17]{0:T(128)S(1)} %pad_add_fusion.info, bf16[8,3,576,256]{3,2,1,0:T(8,128)(2,1)S(1)} %copy-done.1, bf16[8,64,640]{2,1,0:T(8,128)(2,1)S(1)} %copy-done.3, bf16[8,64,640]{2,1,0:T(8,128)(2,1)S(1)} %collective-permute-done.4.refs_1_.refs_2_, bf16[9,2,640]{2,1,0:T(2,128)(2,1)S(1)} %bitcast.5), custom_call_target="tpu_custom_call" | custom-call | flops 2684354560 | bytes 5242880 | tf_op jit(solution)/shard_map/conv_inner/pallas_call | solution.py:229
  36.8 0.0 collective-permute-done.1.far_body
  36.8 0.0 slice-done
  36.8 0.0 slice-done.1
  36.9 0.0 copy-done.5
  36.9 0.0 copy-done.6
  36.9 4.8 %finish.2 = (bf16[8,64,640]{2,1,0:T(8,128)(2,1)S(1)}, bf16[2,64,640]{2,1,0:T(8,128)(2,1)S(1)}, bf16[1,64,640]{2,1,0:T(8,128)(2,1)S(1)}, bf16[3,64,640]{2,1,0:T(8,128)(2,1)S(1)}, bf16[5,64,640]{2,1,0:T(8,128)(2,1)S(1)}) custom-call(bf16[8,3,576,256]{3,2,1,0:T(8,128)(2,1)S(1)} %bitcast.3, bf16[3,64,640]{2,1,0:T(8,128)(2,1)S(1)} %collective-permute-done.far_edge, ...), custom_call_target="tpu_custom_call" | custom-call | flops 5368709120 | bytes 8388608 | tf_op jit(solution)/shard_map/finish/pallas_call | solution.py:309
  41.7 0.1 collective-permute-start.14
  41.8 1.5 %collective-permute-start.13 = (bf16[2,64,640]{2,1,0:T(8,128)(2,1)S(1)}, bf16[2,64,640]{2,1,0:T(8,128)(2,1)S(1)}, u32[]{:S(2)}, u32[]{:S(2)}) collective-permute-start(bf16[2,64,640]{2,1,0:T(8,128)(2,1)S(1)} %get-tuple-element.21), channel_id=1, source_target_pairs={{0,8},{8,16},{16,24},{24,0},{1,9},{9,17},{17,25},{25,1},{2,10},{10... | collective-permute-start | bytes 491528 | tf_op jit(solution)/shard_map/ppermute | solution.py:357
  43.2 0.8 %collective-permute-start.8 = (bf16[3,64,640]{2,1,0:T(8,128)(2,1)S(1)}, bf16[3,64,640]{2,1,0:T(8,128)(2,1)S(1)}, u32[]{:S(2)}, u32[]{:S(2)}) collective-permute-start(bf16[3,64,640]{2,1,0:T(8,128)(2,1)S(1)} %get-tuple-element.18), channel_id=1, source_target_pairs={{0,7},{1,2},{2,1},{3,4},{4,3},{5,6},{6,5},{7,0},{8,15},{9,10},{10,... | collective-permute-start | bytes 737288 | tf_op jit(solution)/shard_map/ppermute | solution.py:354
  44.1 0.9 %collective-permute-start.9 = (bf16[5,64,640]{2,1,0:T(8,128)(2,1)S(1)}, bf16[5,64,640]{2,1,0:T(8,128)(2,1)S(1)}, u32[]{:S(2)}, u32[]{:S(2)}) collective-permute-start(bf16[5,64,640]{2,1,0:T(8,128)(2,1)S(1)} %get-tuple-element.19), channel_id=1, source_target_pairs={{0,7},{1,2},{2,1},{3,4},{4,3},{5,6},{6,5},{7,0},{8,15},{9,10},{10,... | collective-permute-start | bytes 1228808 | tf_op jit(solution)/shard_map/ppermute | solution.py:355
  45.0 3.2 %collective-permute-start.12 = (bf16[8,64,640]{2,1,0:T(8,128)(2,1)S(1)}, bf16[8,64,640]{2,1,0:T(8,128)(2,1)S(1)}, u32[]{:S(2)}, u32[]{:S(2)}) collective-permute-start(bf16[8,64,640]{2,1,0:T(8,128)(2,1)S(1)} %get-tuple-element.20.refs_0_.field), channel_id=1, source_target_pairs={{0,1},{1,0},{2,3},{3,2},{4,5},{5,4},{6,7},{7,6},{8,9},{9,8},{10,11... | collective-permute-start | bytes 1966088 | tf_op jit(solution)/shard_map/ppermute | solution.py:356
  48.2 0.0 collective-permute-done.14
  48.2 0.7 collective-permute-done.13
  49.0 0.3 collective-permute-done.8.far_edge
  49.3 1.3 %collective-permute-start.11 = (bf16[1,64,640]{2,1,0:T(8,128)(2,1)S(1)}, bf16[1,64,640]{2,1,0:T(8,128)(2,1)S(1)}, u32[]{:S(2)}, u32[]{:S(2)}) collective-permute-start(bf16[1,64,640]{2,1,0:T(8,128)(2,1)S(1)} %slice.19), channel_id=1, source_target_pairs={{0,24},{8,0},{16,8},{24,16},{1,25},{9,1},{17,9},{25,17},{2,26},{10... | collective-permute-start | bytes 245768 | tf_op jit(solution)/shard_map/ppermute | solution.py:363
  50.6 5.3 %collective-permute-start.15 = (bf16[3,64,640]{2,1,0:T(8,128)(2,1)S(1)}, bf16[3,64,640]{2,1,0:T(8,128)(2,1)S(1)}, u32[]{:S(2)}, u32[]{:S(2)}) collective-permute-start(bf16[3,64,640]{2,1,0:T(8,128)(2,1)S(1)} %pad_maximum_fusion.3.refs_1_), channel_id=1, source_target_pairs={{0,1},{1,0},{2,3},{3,2},{4,5},{5,4},{6,7},{7,6},{8,9},{9,8},{10,11... | collective-permute-start | bytes 737288 | tf_op jit(solution)/shard_map/ppermute | solution.py:365
  55.9 0.8 %collective-permute-start.10 = (bf16[2,64,640]{2,1,0:T(8,128)(2,1)S(1)}, bf16[2,64,640]{2,1,0:T(8,128)(2,1)S(1)}, u32[]{:S(2)}, u32[]{:S(2)}) collective-permute-start(bf16[2,64,640]{2,1,0:T(8,128)(2,1)S(1)} %slice.18), channel_id=1, source_target_pairs={{0,8},{8,16},{16,24},{24,0},{1,9},{9,17},{17,25},{25,1},{2,10},{10... | collective-permute-start | bytes 491528 | tf_op jit(solution)/shard_map/ppermute | solution.py:362
  56.7 0.0 collective-permute-done.11
  56.7 5.8 %collective-permute-done.10 = bf16[2,64,640]{2,1,0:T(8,128)(2,1)S(1)} collective-permute-done((bf16[2,64,640]{2,1,0:T(8,128)(2,1)S(1)}, bf16[2,64,640]{2,1,0:T(8,128)(2,1)S(1)}, u32[]{:S(2)}, u32[]{:S(2)}) %collective-permute-start.10) | collective-permute-done | bytes 163872 | tf_op jit(solution)/shard_map/ppermute | solution.py:362
  62.6 0.0 collective-permute-done.15.refs_3_
  62.6 0.0 collective-permute-done.12.refs_1_.refs_2_
  62.6 2.7 %conv_outer.3.part_outer = f32[3,64,640]{2,1,0:T(8,128)S(1)} custom-call(s32[17]{0:T(128)S(1)} %pad_add_fusion.info, bf16[8,3,576,256]{3,2,1,0:T(8,128)(2,1)S(1)} %bitcast.3, bf16[8,64,640]{2,1,0:T(8,128)(2,1)S(1)} %get-tuple-element.20.refs_0_.field, bf16[3,64,640]{2,1,0:T(8,128)(2,1)S(1)} %pad_maximum_fusion.3.refs_1_, ...), custom_call_target="tpu_custom_call" | custom-call | flops 1610612736 | bytes 3145728 | tf_op jit(solution)/shard_map/conv_outer/pallas_call | solution.py:229
  65.3 3.9 %conv_inner.3.part_inner = f32[5,64,640]{2,1,0:T(8,128)S(1)} custom-call(s32[17]{0:T(128)S(1)} %pad_add_fusion.info, bf16[8,3,576,256]{3,2,1,0:T(8,128)(2,1)S(1)} %bitcast.3, bf16[8,64,640]{2,1,0:T(8,128)(2,1)S(1)} %get-tuple-element.20.refs_0_.field, bf16[8,64,640]{2,1,0:T(8,128)(2,1)S(1)} %collective-permute-done.12.refs_1_.refs_2_, ...), custom_call_target="tpu_custom_call" | custom-call | flops 2684354560 | bytes 5242880 | tf_op jit(solution)/shard_map/conv_inner/pallas_call | solution.py:229
  69.2 0.0 collective-permute-done.9.far_body
  69.2 5.5 %finish.3 = bf16[8,64,640]{2,1,0:T(8,128)(2,1)} custom-call(bf16[8,3,576,256]{3,2,1,0:T(8,128)(2,1)S(1)} %bitcast.3, bf16[3,64,640]{2,1,0:T(8,128)(2,1)S(1)} %collective-permute-done.8.far_edge, bf16[5,64,640]{2,1,0:T(8,128)(2,1)S(1)} %collective-permute-done.9.far_body, bf16[3,64,640]{2,1,0:T(8,128)(2,1)S(1)} %pad_maximum_fusion.2.far_halo, ...), custom_call_target="tpu_custom_call" | custom-call | flops 5368709120 | bytes 8388608 | tf_op jit(solution)/shard_map/finish/pallas_call | solution.py:309
  (20 shorter events, 0.3 us)
Async XLA Ops:
  0.0 27.3 %collective-permute-start.4 = (bf16[8,64,640]{2,1,0:T(8,128)(2,1)}, bf16[8,64,640]{2,1,0:T(8,128)(2,1)S(1)}, u32[]{:S(2)}, u32[]{:S(2)}) collective-permute-start(bf16[8,64,640]{2,1,0:T(8,128)(2,1)} %field.3), channel_id=1, source_target_pairs={{0,1},{1,0},{2,3},{3,2},{4,5},{5,4},{6,7},{7,6},{8,9},{9,8},{10,11... | collective-permute-start | bytes 1966088 | tf_op jit(solution)/shard_map/ppermute | solution.py:356
  0.0 1.1 %copy-start.2 = (bf16[8,64,640]{2,1,0:T(8,128)(2,1)S(1)}, bf16[8,64,640]{2,1,0:T(8,128)(2,1)}, u32[]{:S(2)}) copy-start(bf16[8,64,640]{2,1,0:T(8,128)(2,1)} %field.3) | copy-start | bytes 1966084
  2.0 13.3 %collective-permute-start.6 = (bf16[1,64,640]{2,1,0:T(8,128)(2,1)S(1)}, bf16[1,64,640]{2,1,0:T(8,128)(2,1)S(1)}, u32[]{:S(2)}, u32[]{:S(2)}) collective-permute-start(bf16[1,64,640]{2,1,0:T(8,128)(2,1)S(1)} %get-tuple-element.17), channel_id=1, source_target_pairs={{0,24},{8,0},{16,8},{24,16},{1,25},{9,1},{17,9},{25,17},{2,26},{10... | collective-permute-start | bytes 245768 | tf_op jit(solution)/shard_map/ppermute | solution.py:358
  5.7 9.6 %collective-permute-start.5 = (bf16[2,64,640]{2,1,0:T(8,128)(2,1)S(1)}, bf16[2,64,640]{2,1,0:T(8,128)(2,1)S(1)}, u32[]{:S(2)}, u32[]{:S(2)}) collective-permute-start(bf16[2,64,640]{2,1,0:T(8,128)(2,1)S(1)} %get-tuple-element.16), channel_id=1, source_target_pairs={{0,8},{8,16},{16,24},{24,0},{1,9},{9,17},{17,25},{25,1},{2,10},{10... | collective-permute-start | bytes 491528 | tf_op jit(solution)/shard_map/ppermute | solution.py:357
  5.7 9.6 %collective-permute-start = (bf16[3,64,640]{2,1,0:T(8,128)(2,1)S(1)}, bf16[3,64,640]{2,1,0:T(8,128)(2,1)S(1)}, u32[]{:S(2)}, u32[]{:S(2)}) collective-permute-start(bf16[3,64,640]{2,1,0:T(8,128)(2,1)S(1)} %get-tuple-element.14), channel_id=1, source_target_pairs={{0,7},{1,2},{2,1},{3,4},{4,3},{5,6},{6,5},{7,0},{8,15},{9,10},{10,... | collective-permute-start | bytes 737288 | tf_op jit(solution)/shard_map/ppermute | solution.py:354
  7.1 29.7 %collective-permute-start.1 = (bf16[5,64,640]{2,1,0:T(8,128)(2,1)S(1)}, bf16[5,64,640]{2,1,0:T(8,128)(2,1)S(1)}, u32[]{:S(2)}, u32[]{:S(2)}) collective-permute-start(bf16[5,64,640]{2,1,0:T(8,128)(2,1)S(1)} %get-tuple-element.15), channel_id=1, source_target_pairs={{0,7},{1,2},{2,1},{3,4},{4,3},{5,6},{6,5},{7,0},{8,15},{9,10},{10,... | collective-permute-start | bytes 1228808 | tf_op jit(solution)/shard_map/ppermute | solution.py:355
  8.4 0.9 %copy-start.7 = (bf16[8,9,4,129]{3,2,1,0:T(4,128)(2,1)S(1)}, bf16[8,9,4,129]{3,2,1,0:T(4,128)(2,1)}, u32[]{:S(2)}) copy-start(bf16[8,9,4,129]{3,2,1,0:T(4,128)(2,1)} %taps.1) | copy-start | bytes 222916
  9.3 18.0 %copy-start.3 = (bf16[8,64,640]{2,1,0:T(8,128)(2,1)S(1)}, bf16[8,64,640]{2,1,0:T(8,128)(2,1)}, u32[]{:S(2)}) copy-start(bf16[8,64,640]{2,1,0:T(8,128)(2,1)} %field.3) | copy-start | bytes 1966084
  9.3 18.0 %copy-start.4 = (bf16[2,9,640]{2,0,1:T(2,128)(2,1)S(1)}, bf16[2,9,640]{2,0,1:T(2,128)(2,1)}, u32[]{:S(2)}) copy-start(bf16[2,9,640]{2,0,1:T(2,128)(2,1)} %param.11) | copy-start | bytes 69124
  12.4 2.9 %copy-start = (bf16[8,3,576,256]{3,2,1,0:T(8,128)(2,1)}, bf16[8,3,576,256]{3,2,1,0:T(8,128)(2,1)S(1)}, u32[]{:S(2)}) copy-start(bf16[8,3,576,256]{3,2,1,0:T(8,128)(2,1)S(1)} %bands.1.band) | copy-start | bytes 21233668
  15.3 5.2 %collective-permute-start.3 = (bf16[1,64,640]{2,1,0:T(8,128)(2,1)S(1)}, bf16[1,64,640]{2,1,0:T(8,128)(2,1)S(1)}, u32[]{:S(2)}, u32[]{:S(2)}) collective-permute-start(bf16[1,64,640]{2,1,0:T(8,128)(2,1)S(1)} %slice.17), channel_id=1, source_target_pairs={{0,24},{8,0},{16,8},{24,16},{1,25},{9,1},{17,9},{25,17},{2,26},{10... | collective-permute-start | bytes 245768 | tf_op jit(solution)/shard_map/ppermute | solution.py:363
  17.8 9.5 %collective-permute-start.7 = (bf16[3,64,640]{2,1,0:T(8,128)(2,1)S(1)}, bf16[3,64,640]{2,1,0:T(8,128)(2,1)S(1)}, u32[]{:S(2)}, u32[]{:S(2)}) collective-permute-start(bf16[3,64,640]{2,1,0:T(8,128)(2,1)S(1)} %pad_maximum_fusion.1.refs_1_), channel_id=1, source_target_pairs={{0,1},{1,0},{2,3},{3,2},{4,5},{5,4},{6,7},{7,6},{8,9},{9,8},{10,11... | collective-permute-start | bytes 737288 | tf_op jit(solution)/shard_map/ppermute | solution.py:365
  20.5 6.7 %collective-permute-start.2 = (bf16[2,64,640]{2,1,0:T(8,128)(2,1)S(1)}, bf16[2,64,640]{2,1,0:T(8,128)(2,1)S(1)}, u32[]{:S(2)}, u32[]{:S(2)}) collective-permute-start(bf16[2,64,640]{2,1,0:T(8,128)(2,1)S(1)} %slice.16), channel_id=1, source_target_pairs={{0,8},{8,16},{16,24},{24,0},{1,9},{9,17},{17,25},{25,1},{2,10},{10... | collective-permute-start | bytes 491528 | tf_op jit(solution)/shard_map/ppermute | solution.py:362
  27.3 3.0 %copy-start.1 = (bf16[8,3,576,256]{3,2,1,0:T(8,128)(2,1)S(1)}, bf16[8,3,576,256]{3,2,1,0:T(8,128)(2,1)}, u32[]{:S(2)}) copy-start(bf16[8,3,576,256]{3,2,1,0:T(8,128)(2,1)} %copy-done) | copy-start | bytes 21233668
  30.3 6.5 %slice-start = ((s8[7077888]{0:T(1024)(128)(4,1)}), s8[4194304]{0:T(1024)(128)(4,1)S(1)}, s32[]{:S(2)}) async-start(s8[7077888]{0:T(1024)(128)(4,1)} %bitcast.2), calls=%async_computation | async-start | bytes 8388608
  33.0 3.9 %slice-start.1 = ((s8[7077888]{0:T(1024)(128)(4,1)}), s8[2883584]{0:T(1024)(128)(4,1)S(1)}, s32[]{:S(2)}) async-start(s8[7077888]{0:T(1024)(128)(4,1)} %bitcast.2), calls=%async_computation.1 | async-start | bytes 5767168
  33.0 3.9 %copy-start.5 = (bf16[2,640,1280]{2,1,0:T(8,128)(2,1)S(1)}, bf16[2,640,1280]{2,1,0:T(8,128)(2,1)}, u32[]{:S(2)}) copy-start(bf16[2,640,1280]{2,1,0:T(8,128)(2,1)} %first.3) | copy-start | bytes 9830404
  33.0 3.9 %copy-start.6 = (bf16[2,1280,640]{2,1,0:T(8,128)(2,1)S(1)}, bf16[2,1280,640]{2,1,0:T(8,128)(2,1)}, u32[]{:S(2)}) copy-start(bf16[2,1280,640]{2,1,0:T(8,128)(2,1)} %second.3) | copy-start | bytes 9830404
  41.7 6.5 %collective-permute-start.14 = (bf16[1,64,640]{2,1,0:T(8,128)(2,1)S(1)}, bf16[1,64,640]{2,1,0:T(8,128)(2,1)S(1)}, u32[]{:S(2)}, u32[]{:S(2)}) collective-permute-start(bf16[1,64,640]{2,1,0:T(8,128)(2,1)S(1)} %get-tuple-element.22), channel_id=1, source_target_pairs={{0,24},{8,0},{16,8},{24,16},{1,25},{9,1},{17,9},{25,17},{2,26},{10... | collective-permute-start | bytes 245768 | tf_op jit(solution)/shard_map/ppermute | solution.py:358
  41.8 7.2 %collective-permute-start.13 = (bf16[2,64,640]{2,1,0:T(8,128)(2,1)S(1)}, bf16[2,64,640]{2,1,0:T(8,128)(2,1)S(1)}, u32[]{:S(2)}, u32[]{:S(2)}) collective-permute-start(bf16[2,64,640]{2,1,0:T(8,128)(2,1)S(1)} %get-tuple-element.21), channel_id=1, source_target_pairs={{0,8},{8,16},{16,24},{24,0},{1,9},{9,17},{17,25},{25,1},{2,10},{10... | collective-permute-start | bytes 491528 | tf_op jit(solution)/shard_map/ppermute | solution.py:357
  43.2 6.0 %collective-permute-start.8 = (bf16[3,64,640]{2,1,0:T(8,128)(2,1)S(1)}, bf16[3,64,640]{2,1,0:T(8,128)(2,1)S(1)}, u32[]{:S(2)}, u32[]{:S(2)}) collective-permute-start(bf16[3,64,640]{2,1,0:T(8,128)(2,1)S(1)} %get-tuple-element.18), channel_id=1, source_target_pairs={{0,7},{1,2},{2,1},{3,4},{4,3},{5,6},{6,5},{7,0},{8,15},{9,10},{10,... | collective-permute-start | bytes 737288 | tf_op jit(solution)/shard_map/ppermute | solution.py:354
  44.1 25.1 %collective-permute-start.9 = (bf16[5,64,640]{2,1,0:T(8,128)(2,1)S(1)}, bf16[5,64,640]{2,1,0:T(8,128)(2,1)S(1)}, u32[]{:S(2)}, u32[]{:S(2)}) collective-permute-start(bf16[5,64,640]{2,1,0:T(8,128)(2,1)S(1)} %get-tuple-element.19), channel_id=1, source_target_pairs={{0,7},{1,2},{2,1},{3,4},{4,3},{5,6},{6,5},{7,0},{8,15},{9,10},{10,... | collective-permute-start | bytes 1228808 | tf_op jit(solution)/shard_map/ppermute | solution.py:355
  45.0 17.6 %collective-permute-start.12 = (bf16[8,64,640]{2,1,0:T(8,128)(2,1)S(1)}, bf16[8,64,640]{2,1,0:T(8,128)(2,1)S(1)}, u32[]{:S(2)}, u32[]{:S(2)}) collective-permute-start(bf16[8,64,640]{2,1,0:T(8,128)(2,1)S(1)} %get-tuple-element.20.refs_0_.field), channel_id=1, source_target_pairs={{0,1},{1,0},{2,3},{3,2},{4,5},{5,4},{6,7},{7,6},{8,9},{9,8},{10,11... | collective-permute-start | bytes 1966088 | tf_op jit(solution)/shard_map/ppermute | solution.py:356
  49.3 7.4 %collective-permute-start.11 = (bf16[1,64,640]{2,1,0:T(8,128)(2,1)S(1)}, bf16[1,64,640]{2,1,0:T(8,128)(2,1)S(1)}, u32[]{:S(2)}, u32[]{:S(2)}) collective-permute-start(bf16[1,64,640]{2,1,0:T(8,128)(2,1)S(1)} %slice.19), channel_id=1, source_target_pairs={{0,24},{8,0},{16,8},{24,16},{1,25},{9,1},{17,9},{25,17},{2,26},{10... | collective-permute-start | bytes 245768 | tf_op jit(solution)/shard_map/ppermute | solution.py:363
  50.6 12.0 %collective-permute-start.15 = (bf16[3,64,640]{2,1,0:T(8,128)(2,1)S(1)}, bf16[3,64,640]{2,1,0:T(8,128)(2,1)S(1)}, u32[]{:S(2)}, u32[]{:S(2)}) collective-permute-start(bf16[3,64,640]{2,1,0:T(8,128)(2,1)S(1)} %pad_maximum_fusion.3.refs_1_), channel_id=1, source_target_pairs={{0,1},{1,0},{2,3},{3,2},{4,5},{5,4},{6,7},{7,6},{8,9},{9,8},{10,11... | collective-permute-start | bytes 737288 | tf_op jit(solution)/shard_map/ppermute | solution.py:365
  55.9 6.7 %collective-permute-start.10 = (bf16[2,64,640]{2,1,0:T(8,128)(2,1)S(1)}, bf16[2,64,640]{2,1,0:T(8,128)(2,1)S(1)}, u32[]{:S(2)}, u32[]{:S(2)}) collective-permute-start(bf16[2,64,640]{2,1,0:T(8,128)(2,1)S(1)} %slice.18), channel_id=1, source_target_pairs={{0,8},{8,16},{16,24},{24,0},{1,9},{9,17},{17,25},{25,1},{2,10},{10... | collective-permute-start | bytes 491528 | tf_op jit(solution)/shard_map/ppermute | solution.py:362
